TPU v7x, 32 devices: a whole 2x2x4 slice. The times are simulated.
32 devices in a mesh: grp: 4 (over y, x), mem: 8 (over z, core).
Axes of the slice: x: 2, y: 2, z: 4, core: 2. Of those that a mesh axis runs over, the one named last changes fastest.
Arguments:
- factors: bfloat16 [32, 512, 2048], P(('grp', 'mem')), may hold values from -1 to 1
- occ_energy: bfloat16 [32], P(('grp', 'mem')), may hold values from -1.5 to -0.29882812
- vir_energy: bfloat16 [512], replicated, may hold values from 0.3984375 to 3
- pair_code: int32 [4, 8, 3], P('grp'), may hold values from 0 to 2
- pair_count: int32 [4, 8], P('grp'), may hold values from 1 to 3
Outputs:
- aux_density: bfloat16 [32, 512, 2048], P(('grp', 'mem'))
- lagrangian: bfloat16 [32, 512, 2048], P(('grp', 'mem'))
Inputs may be any that keep to these rules, and one draw needn't show every extreme that they name: `pair_code`: only the first pair_count entries of a device's list are read; entries may repeat.
All inputs are finite; a program needn't handle non-finite values.
Results may differ from a plain program's by a relative error of at most 0.0056.
Values may be sent and summed in bfloat16 or wider, within the bound.
No kernel may reach another device: no remote copies, remote signals or barrier semaphores. Data moves between devices by JAX's collectives and lax.ppermute only.
A program may use at most 128 MiB of HBM per device.

v0:
```python
import jax
import jax.numpy as jnp
from jax import lax
from jax.experimental import pallas as pl
from jax.experimental.pallas import tpu as pltpu
from jax.sharding import PartitionSpec as P


STRIPS = 4
TILE = 128
F32 = jnp.float32
BF16 = jnp.bfloat16

VMEM = pl.BlockSpec(memory_space=pltpu.VMEM)
SMEM = pl.BlockSpec(memory_space=pltpu.SMEM)


def leads(member):
    return (member & 1) == ((member >> 1) & 1)


def first_round(member):
    return jnp.where(leads(member), 2, 1)


def turn(value, back):
    pairs = []
    for member in range(lax.axis_size("mem")):
        target = member ^ (1 if leads(member) else 2)
        pairs.append((target, member) if back else (member, target))
    return lax.ppermute(value, "mem", pairs)


def swap(value, masks):
    groups, members = lax.axis_size("grp"), lax.axis_size("mem")
    pairs = []
    for g in range(groups):
        for m in range(members):
            grp_mask, mem_mask = masks[0] if leads(m) else masks[1]
            pairs.append((g * members + m, (g ^ grp_mask) * members + (m ^ mem_mask)))
    return lax.ppermute(value, ("grp", "mem"), pairs)


def live(codes, counts, member, round_no):
    total = jnp.int32(0)
    for slot in range(codes.shape[2]):
        hit = (slot < counts[0, member]) & (codes[0, member, slot] == round_no)
        total = total + hit.astype(jnp.int32)
    return total


def weights(codes, counts, round_no):
    me = lax.axis_index("mem")
    other = jnp.where(round_no == 0, me, me ^ round_no)
    own = live(codes, counts, me, round_no)
    far = live(codes, counts, other, round_no)
    return own.astype(F32), far.astype(F32)


def nt(a, b):
    return lax.dot_general(a, b, (((1,), (1,)), ((), ())), preferred_element_type=F32)


def nn(a, b):
    return jnp.dot(a, b, preferred_element_type=F32)


def early_kernel(b_ref, row_ref, e_ref, codes, counts, base_ref, dens_ref, gamma_ref, amp):
    vir, aux = b_ref.shape
    row = row_ref[...]
    col = jnp.broadcast_to(row, (vir, vir)).T
    base_ref[...] = col + row
    own, _ = weights(codes, counts, 0)
    energy = e_ref[0]
    half = vir // 2
    for at in (slice(0, half), slice(half, vir)):
        k = nt(b_ref[...], b_ref[at, :])
        amp[:, at] = (k / (base_ref[:, at] - energy - energy)).astype(BF16)
    a = amp[...]
    dens_ref[...] = own * nn(a, a)
    for p in range(STRIPS):
        at = pl.ds(p * (aux // STRIPS), aux // STRIPS)
        gamma_ref[:, at] = (2.0 * own) * nn(a, b_ref[:, at])


def amp_part(at, b_ref, r_ref, base_ref, e_ref, far_ref):
    k = nt(b_ref[...], r_ref[...])
    return (k / (base_ref[:, at] - e_ref[0] - far_ref[0])).astype(BF16)


def blocks(size):
    count = size // TILE
    return [(i, j) for i in range(count) for j in range(i, count)]


def density_kernel(b_ref, r_ref, base_ref, e_ref, far_ref, codes, counts, dens_in, mt_ref, keep_ref, send_ref, m_ref):
    vir = b_ref.shape[0]
    half = vir // 2
    me = lax.axis_index("mem")
    own, far = weights(codes, counts, first_round(me))
    for at in (slice(0, half), slice(half, vir)):
        mt = amp_part(at, b_ref, r_ref.at[at, :], base_ref, e_ref, far_ref)
        mt_ref[:, at] = mt
        m_ref[at, :] = mt.T
    high, low = slice(0, half), slice(half, vir)

    def sums(rows, columns):
        one = nn(mt_ref[rows, :], m_ref[:, columns])
        two = nn(m_ref[rows, :], mt_ref[:, columns])
        return dens_in[rows, columns] + own * one + far * two

    top, rest = sums(high, slice(0, vir)), sums(low, low)
    pieces = []
    for i, j in blocks(vir):
        if i * TILE < half:
            pieces.append(top[i * TILE : (i + 1) * TILE, j * TILE : (j + 1) * TILE])
        else:
            a, b = i * TILE - half, j * TILE - half
            pieces.append(rest[a : a + TILE, b : b + TILE])
    lead = leads(me)
    count = len(pieces) // 2
    for n in range(count):
        at = pl.ds(n * TILE, TILE)
        keep_ref[at, :] = jnp.where(lead, pieces[n], pieces[n + count])
        send_ref[at, :] = jnp.where(lead, pieces[n + count], pieces[n]).astype(BF16)


def first_gamma_kernel(codes, counts, gamma_in, mt_ref, r_ref, gamma_ref):
    own, far = weights(codes, counts, first_round(lax.axis_index("mem")))
    aux = gamma_ref.shape[1]
    for p in range(STRIPS):
        at = pl.ds(p * (aux // STRIPS), aux // STRIPS)
        gamma_ref[:, at] = gamma_in[:, at] + (own + far) * nn(mt_ref[...], r_ref[:, at])


def strips_out(out_ref, held, sems, compute):
    step = held.shape[1] // STRIPS
    copies = []
    for p in range(STRIPS):
        at = pl.ds(p * step, step)
        held[:, at] = compute(at).astype(held.dtype)
        copies.append(pltpu.make_async_copy(held.at[:, at], out_ref.at[:, at], sems.at[p]))
        copies[-1].start()
    for copy in copies:
        copy.wait()


def last_gamma_kernel(
    codes, counts, b_ref, ra_ref, rb_ref, base_ref, e_ref, far_ref, gamma_in, out_ref, held, mt_ref, sems
):
    own, far = weights(codes, counts, 3 - first_round(lax.axis_index("mem")))
    vir, cut = b_ref.shape[0], ra_ref.shape[0]
    for at, r_ref in ((slice(0, cut), ra_ref), (slice(cut, vir), rb_ref)):
        mt_ref[:, at] = amp_part(at, b_ref, r_ref, base_ref, e_ref, far_ref)

    def strip(at):
        total = nn(mt_ref[:, :cut], ra_ref[:, at]) + nn(mt_ref[:, cut:], rb_ref[:, at])
        return gamma_in[:, at] + (own + far) * total

    strips_out(out_ref, held, sems, strip)


def apply_kernel(mine_ref, other_ref, b_ref, out_ref, tile, held, sems):
    lead = leads(lax.axis_index("mem"))
    names = blocks(tile.shape[0])
    half = len(names) // 2
    for n, (i, j) in enumerate(names):
        at = pl.ds((n % half) * TILE, TILE)
        low, high = (mine_ref, other_ref) if n < half else (other_ref, mine_ref)
        block = jnp.where(lead, low[at, :].astype(F32), high[at, :].astype(F32)).astype(BF16)
        tile[pl.ds(i * TILE, TILE), pl.ds(j * TILE, TILE)] = block
        if i != j:
            tile[pl.ds(j * TILE, TILE), pl.ds(i * TILE, TILE)] = block.T
    strips_out(out_ref, held, sems, lambda at: nn(tile[...], b_ref[:, at]))


def call(kernel, outs, scratch=(), smem=(), count=0, flops=0, out_spec=VMEM):
    return lambda *args: kernel_call(kernel, outs, scratch, smem, count, flops, out_spec)(*args)


def kernel_call(kernel, outs, scratch, smem, count, flops, out_spec):
    return pl.pallas_call(
        kernel,
        out_shape=outs,
        in_specs=[SMEM if i in smem else VMEM for i in range(count)],
        out_specs=jax.tree.map(lambda _: out_spec, outs),
        scratch_shapes=scratch,
        compiler_params=pltpu.CompilerParams(vmem_limit_bytes=32 << 20),
        cost_estimate=pl.CostEstimate(flops=flops, bytes_accessed=1 << 20, transcendentals=0),
    )


def per_device(factors, occ_energy, vir_energy, pair_code, pair_count):
    return body(factors[0], occ_energy, vir_energy, pair_code, pair_count)


def body(block, occ_energy, vir_energy, pair_code, pair_count):
    vir, aux = block.shape
    members, groups = lax.axis_size("mem"), lax.axis_size("grp")
    shape = jax.ShapeDtypeStruct
    square = shape((vir, vir), F32)
    wide = shape((vir, aux), F32)
    dot = 2 * vir * vir * aux
    out_scratch = [pltpu.VMEM((vir, aux), BF16), pltpu.SemaphoreType.DMA((STRIPS,))]
    any_space = pl.BlockSpec(memory_space=pl.ANY)

    first_energy = turn(occ_energy, False).astype(F32)
    first = turn(block, False)

    energy = occ_energy.astype(F32)
    row = vir_energy.astype(F32).reshape(1, vir)
    base, dens, gamma = call(
        early_kernel, (square, square, wide), [pltpu.VMEM((vir, vir), BF16)], (2, 3, 4), 5, 2 * dot
    )(block, row, energy, pair_code, pair_count)

    half = len(blocks(vir)) * TILE // 2
    mt, keep, send = call(
        density_kernel,
        (shape((vir, vir), BF16), shape((half, TILE), F32), shape((half, TILE), BF16)),
        [pltpu.VMEM((vir, vir), BF16)], (3, 4, 5, 6), 8, dot,
    )(block, first, base, energy, first_energy, pair_code, pair_count, dens)

    total = keep + swap(send, [(0, 1), (0, 1)]).astype(F32)
    near = [(0, 3)]
    along = [(0, (1 << k) | 3) for k in range(2, members.bit_length() - 1)]
    across = [(1 << k, 0) for k in range(groups.bit_length() - 1)]
    for masks in zip(near + across + along, near + along + across):
        got = swap(total.astype(BF16), masks)
        total = total + got.astype(F32)
    mine = (total * (1.0 / (8.0 * groups * members))).astype(BF16)
    other = swap(mine, [(0, 1), (0, 1)])

    second_energy = turn(occ_energy, True).astype(F32)
    cut = vir // 4
    parta, partb = block[:cut], block[cut:]
    seconda = turn(parta, True)
    secondb = turn(partb, True)
    gamma = call(first_gamma_kernel, wide, (), (0, 1), 5, dot)(
        pair_code, pair_count, gamma, mt, first
    )
    result = call(
        last_gamma_kernel, shape((vir, aux), BF16),
        [out_scratch[0], pltpu.VMEM((vir, vir), BF16), out_scratch[1]],
        (0, 1, 6, 7), 9, 2 * dot, any_space,
    )(pair_code, pair_count, block, seconda, secondb, base, energy, second_energy, gamma)
    lagrangian = call(
        apply_kernel, shape((vir, aux), BF16), [pltpu.VMEM((vir, vir), BF16), *out_scratch], (), 3, dot,
        any_space,
    )(mine, other, block)
    return (result[None], lagrangian[None])


def solution(mesh):
    in_specs = (
        P(("grp", "mem"), None, None),
        P(("grp", "mem")),
        P(),
        P("grp", None, None),
        P("grp", None),
    )
    out_specs = (P(("grp", "mem"), None, None), P(("grp", "mem"), None, None))
    return jax.shard_map(
        per_device, mesh=mesh, in_specs=in_specs, out_specs=out_specs, check_vma=False
    )
```

profile of v0, /device:TPU:0, one launch (start us, length us, event | category | flops | bytes accessed | tf_op | source)
XLA Modules:
  0.0 75.8 jit_solution(14300906552188011257)
XLA Ops:
  0.6 0.6 collective-permute-start.3
  1.2 2.1 %collective-permute-start.4 = (bf16[1]{0:T(256)(128)(2,1)}, bf16[1]{0:T(256)(128)(2,1)}, u32[]{:S(2)}, u32[]{:S(2)}) collective-permute-start(bf16[1]{0:T(256)(128)(2,1)} %param.6), channel_id=1, source_target_pairs={{0,1},{1,3},{2,0},{3,2},{4,5},{5,7},{6,4},{7,6},{8,9},{9,11},{10,8... | collective-permute-start | bytes 14 | tf_op jit(solution)/shard_map/ppermute | solution.py:31
  4.0 0.8 copy.10.codes
  4.7 0.7 reshape.13
  5.4 0.0 copy-start
  5.4 1.6 %copy-done = bf16[1,512,2048]{2,1,0:T(8,128)(2,1)S(1)} copy-done((bf16[1,512,2048]{2,1,0:T(8,128)(2,1)S(1)}, bf16[1,512,2048]{2,1,0:T(8,128)(2,1)}, u32[]{:S(2)}) %copy-start) | copy-done | bytes 2097176
  7.0 0.0 copy-start.2
  7.0 0.7 copy-done.2
  7.6 3.3 %shard_map.68 = (f32[512,512]{1,0:T(8,128)S(1)}, f32[512,512]{1,0:T(8,128)S(1)}, f32[512,2048]{1,0:T(8,128)S(1)}) custom-call(bf16[512,2048]{1,0:T(8,128)(2,1)S(1)} %bitcast.9, f32[1,512]{1,0:T(1,128)S(1)} %bitcast.13, f32[1]{0:T(128)S(6)} %convert_element_type.40.e_ref, s32[1,8,3]{2,1,0:T(8,128)S(1)} %copy.10.codes, s32[1,8]{1,0:T(1,128)S(1)} %copy-done.2), custom_call_target="tpu_custom_call" | custom-call | flops 2147483648 | bytes 1048576 | tf_op jit(solution)/shard_map/pallas_call | solution.py:178
  11.0 17.1 %collective-permute-done.4 = bf16[1]{0:T(256)(128)(2,1)} collective-permute-done((bf16[1]{0:T(256)(128)(2,1)}, bf16[1]{0:T(256)(128)(2,1)}, u32[]{:S(2)}, u32[]{:S(2)}) %collective-permute-start.4) | collective-permute-done | bytes 34 | tf_op jit(solution)/shard_map/ppermute | solution.py:31
  28.6 0.0 collective-permute-done.3.r_ref
  28.6 2.5 %shard_map.69 = (bf16[512,512]{1,0:T(8,128)(2,1)S(1)}, f32[640,128]{1,0:T(8,128)S(1)}, bf16[640,128]{1,0:T(8,128)(2,1)S(1)}) custom-call(bf16[512,2048]{1,0:T(8,128)(2,1)S(1)} %bitcast.10, bf16[512,2048]{1,0:T(8,128)(2,1)S(1)} %collective-permute-done.3.r_ref, f32[512,512]{1,0:T(8,128)S(1)} %get-tuple-element.8.base_ref, f32[1]{0:T(128)S(6)} %convert_element_type.40.e_ref, ...), custom_call_target="tpu_custom_call" | custom-call | flops 1073741824 | bytes 1048576 | tf_op jit(solution)/shard_map/pallas_call | solution.py:178
  31.1 0.1 collective-permute-start.5
  31.2 1.4 %collective-permute-done.5 = bf16[640,128]{1,0:T(8,128)(2,1)S(1)} collective-permute-done((bf16[640,128]{1,0:T(8,128)(2,1)S(1)}, bf16[640,128]{1,0:T(8,128)(2,1)S(1)}, u32[]{:S(2)}, u32[]{:S(2)}) %collective-permute-start.5) | collective-permute-done | bytes 163872 | tf_op jit(solution)/shard_map/ppermute | solution.py:41
  32.6 0.3 collective-permute-start.6
  32.9 0.1 slice_bitcast_fusion
  33.1 0.0 copy-start.3
  33.1 1.6 %collective-permute-start.1 = (bf16[384,2048]{1,0:T(8,128)(2,1)S(1)}, bf16[384,2048]{1,0:T(8,128)(2,1)S(1)}, u32[]{:S(2)}, u32[]{:S(2)}) collective-permute-start(bf16[384,2048]{1,0:T(8,128)(2,1)S(1)} %slice_bitcast_fusion), channel_id=1, source_target_pairs={{1,0},{3,1},{0,2},{2,3},{5,4},{7,5},{4,6},{6,7},{9,8},{11,9},{8,10... | collective-permute-start | bytes 4718600 | tf_op jit(solution)/shard_map/ppermute | solution.py:31
  34.7 4.2 %collective-permute-done.6 = bf16[640,128]{1,0:T(8,128)(2,1)S(1)} collective-permute-done((bf16[640,128]{1,0:T(8,128)(2,1)S(1)}, bf16[640,128]{1,0:T(8,128)(2,1)S(1)}, u32[]{:S(2)}, u32[]{:S(2)}) %collective-permute-start.6) | collective-permute-done | bytes 163872 | tf_op jit(solution)/shard_map/ppermute | solution.py:41
  38.9 0.1 fusion.3
  39.0 2.0 %collective-permute-start.7 = (bf16[640,128]{1,0:T(8,128)(2,1)S(1)}, bf16[640,128]{1,0:T(8,128)(2,1)S(1)}, u32[]{:S(2)}, u32[]{:S(2)}) collective-permute-start(bf16[640,128]{1,0:T(8,128)(2,1)S(1)} %get-tuple-element.14), channel_id=1, source_target_pairs={{0,8},{1,6},{2,5},{3,11},{4,12},{5,2},{6,1},{7,15},{8,0},{9,14},{1... | collective-permute-start | bytes 491528 | tf_op jit(solution)/shard_map/ppermute | solution.py:41
  41.0 3.4 %collective-permute-done.7 = bf16[640,128]{1,0:T(8,128)(2,1)S(1)} collective-permute-done((bf16[640,128]{1,0:T(8,128)(2,1)S(1)}, bf16[640,128]{1,0:T(8,128)(2,1)S(1)}, u32[]{:S(2)}, u32[]{:S(2)}) %collective-permute-start.7) | collective-permute-done | bytes 163872 | tf_op jit(solution)/shard_map/ppermute | solution.py:41
  44.4 2.0 %collective-permute-start.8 = (bf16[640,128]{1,0:T(8,128)(2,1)S(1)}, bf16[640,128]{1,0:T(8,128)(2,1)S(1)}, u32[]{:S(2)}, u32[]{:S(2)}) collective-permute-start(bf16[640,128]{1,0:T(8,128)(2,1)S(1)} %fusion.1), channel_id=1, source_target_pairs={{0,16},{1,9},{2,10},{3,19},{4,20},{5,13},{6,14},{7,23},{8,24},{9,1... | collective-permute-start | bytes 491528 | tf_op jit(solution)/shard_map/ppermute | solution.py:41
  46.4 2.4 %collective-permute-start = (bf16[128,2048]{1,0:T(8,128)(2,1)S(1)}, bf16[128,2048]{1,0:T(8,128)(2,1)S(1)}, u32[]{:S(2)}, u32[]{:S(2)}) collective-permute-start(bf16[128,2048]{1,0:T(8,128)(2,1)S(1)} %slice_bitcast_fusion.1), channel_id=1, source_target_pairs={{1,0},{3,1},{0,2},{2,3},{5,4},{7,5},{4,6},{6,7},{9,8},{11,9},{8,10... | collective-permute-start | bytes 1572872 | tf_op jit(solution)/shard_map/ppermute | solution.py:31
  48.8 0.9 %collective-permute-done.8 = bf16[640,128]{1,0:T(8,128)(2,1)S(1)} collective-permute-done((bf16[640,128]{1,0:T(8,128)(2,1)S(1)}, bf16[640,128]{1,0:T(8,128)(2,1)S(1)}, u32[]{:S(2)}, u32[]{:S(2)}) %collective-permute-start.8) | collective-permute-done | bytes 163872 | tf_op jit(solution)/shard_map/ppermute | solution.py:41
  49.8 0.1 fusion.2
  49.8 1.5 %collective-permute-start.9 = (bf16[640,128]{1,0:T(8,128)(2,1)S(1)}, bf16[640,128]{1,0:T(8,128)(2,1)S(1)}, u32[]{:S(2)}, u32[]{:S(2)}) collective-permute-start(bf16[640,128]{1,0:T(8,128)(2,1)S(1)} %fusion.2), channel_id=1, source_target_pairs={{0,7},{1,17},{2,18},{3,4},{4,3},{5,21},{6,22},{7,0},{8,15},{9,25},... | collective-permute-start | bytes 491528 | tf_op jit(solution)/shard_map/ppermute | solution.py:41
  51.3 2.9 %collective-permute-start.2 = (bf16[1]{0:T(256)(128)(2,1)}, bf16[1]{0:T(256)(128)(2,1)}, u32[]{:S(2)}, u32[]{:S(2)}) collective-permute-start(bf16[1]{0:T(256)(128)(2,1)} %param.6), channel_id=1, source_target_pairs={{1,0},{3,1},{0,2},{2,3},{5,4},{7,5},{4,6},{6,7},{9,8},{11,9},{8,10... | collective-permute-start | bytes 14 | tf_op jit(solution)/shard_map/ppermute | solution.py:31
  54.2 8.8 %collective-permute-done.2 = bf16[1]{0:T(256)(128)(2,1)} collective-permute-done((bf16[1]{0:T(256)(128)(2,1)}, bf16[1]{0:T(256)(128)(2,1)}, u32[]{:S(2)}, u32[]{:S(2)}) %collective-permute-start.2) | collective-permute-done | bytes 34 | tf_op jit(solution)/shard_map/ppermute | solution.py:31
  63.6 0.0 copy-done.3
  63.6 0.0 copy-start.1
  63.6 1.9 %shard_map.70.gamma_in = f32[512,2048]{1,0:T(8,128)S(1)} custom-call(s32[1,8,3]{2,1,0:T(8,128)S(1)} %copy.10.codes, s32[1,8]{1,0:T(1,128)S(1)} %copy-done.3, f32[512,2048]{1,0:T(8,128)S(1)} %get-tuple-element.9.gamma_in, bf16[512,512]{1,0:T(8,128)(2,1)S(1)} %get-tuple-element.11.mt_ref, bf16[512,2048]{1,0:T(8,128)(2,1)S(1)} %collective-permute-done.3.r_ref), custom_call_target="tpu_custom_call" | custom-call | flops 1073741824 | bytes 1048576 | tf_op jit(solution)/shard_map/pallas_call | solution.py:178
  65.5 2.2 %collective-permute-done.9 = bf16[640,128]{1,0:T(8,128)(2,1)S(1)} collective-permute-done((bf16[640,128]{1,0:T(8,128)(2,1)S(1)}, bf16[640,128]{1,0:T(8,128)(2,1)S(1)}, u32[]{:S(2)}, u32[]{:S(2)}) %collective-permute-start.9) | collective-permute-done | bytes 163872 | tf_op jit(solution)/shard_map/ppermute | solution.py:41
  67.7 0.1 multiply_convert_fusion.mine_ref
  67.7 0.1 collective-permute-start.10
  67.8 0.0 collective-permute-done.ra_ref
  67.8 0.0 collective-permute-done.1.rb_ref
  67.8 0.0 copy-done.1
  67.9 5.8 %shard_map.71 = bf16[512,2048]{1,0:T(8,128)(2,1)} custom-call(s32[1,8,3]{2,1,0:T(8,128)S(1)} %copy.10.codes, s32[1,8]{1,0:T(1,128)S(1)} %copy-done.3, bf16[512,2048]{1,0:T(8,128)(2,1)S(1)} %bitcast.11, bf16[128,2048]{1,0:T(8,128)(2,1)S(1)} %collective-permute-done.ra_ref, bf16[384,2048]{1,0:T(8,128)(2,1)S(1)} %collective-permute-done.1.rb_ref, ...), custom_call_target="tpu_custom_call" | custom-call | flops 2147483648 | bytes 1048576 | tf_op jit(solution)/shard_map/pallas_call | solution.py:178
  73.6 0.0 collective-permute-done.10.other_ref
  73.6 2.1 %shard_map.72 = bf16[512,2048]{1,0:T(8,128)(2,1)} custom-call(bf16[640,128]{1,0:T(8,128)(2,1)S(1)} %multiply_convert_fusion.mine_ref, bf16[640,128]{1,0:T(8,128)(2,1)S(1)} %collective-permute-done.10.other_ref, bf16[512,2048]{1,0:T(8,128)(2,1)S(1)} %bitcast.12), custom_call_target="tpu_custom_call" | custom-call | flops 1073741824 | bytes 1048576 | tf_op jit(solution)/shard_map/pallas_call | solution.py:178
  (3 shorter events, 0.1 us)
Async XLA Ops:
  0.6 28.0 %collective-permute-start.3 = (bf16[512,2048]{1,0:T(8,128)(2,1)}, bf16[512,2048]{1,0:T(8,128)(2,1)S(1)}, u32[]{:S(2)}, u32[]{:S(2)}) collective-permute-start(bf16[512,2048]{1,0:T(8,128)(2,1)} %bitcast.8), channel_id=1, source_target_pairs={{0,1},{1,3},{2,0},{3,2},{4,5},{5,7},{6,4},{7,6},{8,9},{9,11},{10,8... | collective-permute-start | bytes 6291464 | tf_op jit(solution)/shard_map/ppermute | solution.py:31
  1.2 26.9 %collective-permute-start.4 = (bf16[1]{0:T(256)(128)(2,1)}, bf16[1]{0:T(256)(128)(2,1)}, u32[]{:S(2)}, u32[]{:S(2)}) collective-permute-start(bf16[1]{0:T(256)(128)(2,1)} %param.6), channel_id=1, source_target_pairs={{0,1},{1,3},{2,0},{3,2},{4,5},{5,7},{6,4},{7,6},{8,9},{9,11},{10,8... | collective-permute-start | bytes 14 | tf_op jit(solution)/shard_map/ppermute | solution.py:31
  5.4 1.6 %copy-start = (bf16[1,512,2048]{2,1,0:T(8,128)(2,1)S(1)}, bf16[1,512,2048]{2,1,0:T(8,128)(2,1)}, u32[]{:S(2)}) copy-start(bf16[1,512,2048]{2,1,0:T(8,128)(2,1)} %param.5) | copy-start | bytes 6291460
  7.0 0.7 copy-start.2
  31.1 1.5 %collective-permute-start.5 = (bf16[640,128]{1,0:T(8,128)(2,1)S(1)}, bf16[640,128]{1,0:T(8,128)(2,1)S(1)}, u32[]{:S(2)}, u32[]{:S(2)}) collective-permute-start(bf16[640,128]{1,0:T(8,128)(2,1)S(1)} %get-tuple-element.13), channel_id=1, source_target_pairs={{0,1},{1,0},{2,3},{3,2},{4,5},{5,4},{6,7},{7,6},{8,9},{9,8},{10,11... | collective-permute-start | bytes 491528 | tf_op jit(solution)/shard_map/ppermute | solution.py:41
  32.6 6.2 %collective-permute-start.6 = (bf16[640,128]{1,0:T(8,128)(2,1)S(1)}, bf16[640,128]{1,0:T(8,128)(2,1)S(1)}, u32[]{:S(2)}, u32[]{:S(2)}) collective-permute-start(bf16[640,128]{1,0:T(8,128)(2,1)S(1)} %fusion), channel_id=1, source_target_pairs={{0,3},{1,2},{2,1},{3,0},{4,7},{5,6},{6,5},{7,4},{8,11},{9,10},{10,... | collective-permute-start | bytes 491528 | tf_op jit(solution)/shard_map/ppermute | solution.py:41
  33.1 30.5 %copy-start.3 = (s32[1,8]{1,0:T(1,128)S(1)}, s32[1,8]{1,0:T(1,128)}, u32[]{:S(2)}) copy-start(s32[1,8]{1,0:T(1,128)} %counts.7) | copy-start | bytes 100
  33.1 34.8 %collective-permute-start.1 = (bf16[384,2048]{1,0:T(8,128)(2,1)S(1)}, bf16[384,2048]{1,0:T(8,128)(2,1)S(1)}, u32[]{:S(2)}, u32[]{:S(2)}) collective-permute-start(bf16[384,2048]{1,0:T(8,128)(2,1)S(1)} %slice_bitcast_fusion), channel_id=1, source_target_pairs={{1,0},{3,1},{0,2},{2,3},{5,4},{7,5},{4,6},{6,7},{9,8},{11,9},{8,10... | collective-permute-start | bytes 4718600 | tf_op jit(solution)/shard_map/ppermute | solution.py:31
  39.0 5.4 %collective-permute-start.7 = (bf16[640,128]{1,0:T(8,128)(2,1)S(1)}, bf16[640,128]{1,0:T(8,128)(2,1)S(1)}, u32[]{:S(2)}, u32[]{:S(2)}) collective-permute-start(bf16[640,128]{1,0:T(8,128)(2,1)S(1)} %get-tuple-element.14), channel_id=1, source_target_pairs={{0,8},{1,6},{2,5},{3,11},{4,12},{5,2},{6,1},{7,15},{8,0},{9,14},{1... | collective-permute-start | bytes 491528 | tf_op jit(solution)/shard_map/ppermute | solution.py:41
  44.4 5.4 %collective-permute-start.8 = (bf16[640,128]{1,0:T(8,128)(2,1)S(1)}, bf16[640,128]{1,0:T(8,128)(2,1)S(1)}, u32[]{:S(2)}, u32[]{:S(2)}) collective-permute-start(bf16[640,128]{1,0:T(8,128)(2,1)S(1)} %fusion.1), channel_id=1, source_target_pairs={{0,16},{1,9},{2,10},{3,19},{4,20},{5,13},{6,14},{7,23},{8,24},{9,1... | collective-permute-start | bytes 491528 | tf_op jit(solution)/shard_map/ppermute | solution.py:41
  46.4 21.4 %collective-permute-start = (bf16[128,2048]{1,0:T(8,128)(2,1)S(1)}, bf16[128,2048]{1,0:T(8,128)(2,1)S(1)}, u32[]{:S(2)}, u32[]{:S(2)}) collective-permute-start(bf16[128,2048]{1,0:T(8,128)(2,1)S(1)} %slice_bitcast_fusion.1), channel_id=1, source_target_pairs={{1,0},{3,1},{0,2},{2,3},{5,4},{7,5},{4,6},{6,7},{9,8},{11,9},{8,10... | collective-permute-start | bytes 1572872 | tf_op jit(solution)/shard_map/ppermute | solution.py:31
  49.8 17.8 %collective-permute-start.9 = (bf16[640,128]{1,0:T(8,128)(2,1)S(1)}, bf16[640,128]{1,0:T(8,128)(2,1)S(1)}, u32[]{:S(2)}, u32[]{:S(2)}) collective-permute-start(bf16[640,128]{1,0:T(8,128)(2,1)S(1)} %fusion.2), channel_id=1, source_target_pairs={{0,7},{1,17},{2,18},{3,4},{4,3},{5,21},{6,22},{7,0},{8,15},{9,25},... | collective-permute-start | bytes 491528 | tf_op jit(solution)/shard_map/ppermute | solution.py:41
  51.3 11.7 %collective-permute-start.2 = (bf16[1]{0:T(256)(128)(2,1)}, bf16[1]{0:T(256)(128)(2,1)}, u32[]{:S(2)}, u32[]{:S(2)}) collective-permute-start(bf16[1]{0:T(256)(128)(2,1)} %param.6), channel_id=1, source_target_pairs={{1,0},{3,1},{0,2},{2,3},{5,4},{7,5},{4,6},{6,7},{9,8},{11,9},{8,10... | collective-permute-start | bytes 14 | tf_op jit(solution)/shard_map/ppermute | solution.py:31
  63.6 4.3 %copy-start.1 = (bf16[1,512,2048]{2,1,0:T(8,128)(2,1)S(1)}, bf16[1,512,2048]{2,1,0:T(8,128)(2,1)}, u32[]{:S(2)}) copy-start(bf16[1,512,2048]{2,1,0:T(8,128)(2,1)} %param.5) | copy-start | bytes 6291460
  67.7 5.9 %collective-permute-start.10 = (bf16[640,128]{1,0:T(8,128)(2,1)S(1)}, bf16[640,128]{1,0:T(8,128)(2,1)S(1)}, u32[]{:S(2)}, u32[]{:S(2)}) collective-permute-start(bf16[640,128]{1,0:T(8,128)(2,1)S(1)} %multiply_convert_fusion.mine_ref), channel_id=1, source_target_pairs={{0,1},{1,0},{2,3},{3,2},{4,5},{5,4},{6,7},{7,6},{8,9},{9,8},{10,11... | collective-permute-start | bytes 491528 | tf_op jit(solution)/shard_map/ppermute | solution.py:41
where the time goes:
time: 76 us; the launch traced here: 75.8 us
  waiting for transfers between devices  38 us (50%)
  Pallas kernels  15.6 us (21%)
  starting transfers between devices  15.5 us (20%)
  local copies, waits for them, and re-layouts  3.15 us (4%)
  between operations  2.54 us (3%)
  other arithmetic  0.97 us (1%)
    ppermute x5, waiting for transfers between devices, turn(): return lax.ppermute(value, 'mem', pairs)  25.9 us
    pallas_call x5, Pallas kernels, call(): kernel_call(kernel, outs, scratch, smem, count, flops, out_spec)(*args)  15.6 us
    ppermute x6, waiting for transfers between devices, swap(): return lax.ppermute(value, ('grp', 'mem'), pairs)  12.1 us
    ppermute x5, starting transfers between devices, turn(): return lax.ppermute(value, 'mem', pairs)  9.55 us
    ppermute x6, starting transfers between devices, swap(): return lax.ppermute(value, ('grp', 'mem'), pairs)  5.94 us
    unnamed x9, local copies, waits for them, and re-layouts  3.01 us
  transfers between devices with their start and end apart: 11, of which 7 were waited for; matrix products, arithmetic and copies ran while one was open for 2% of the time, Pallas kernels for 14%

commit v1 on v0

--- a/solution.py
+++ b/solution.py
@@ -145,19 +145,28 @@
         copy.wait()
 
 
-def last_gamma_kernel(
-    codes, counts, b_ref, ra_ref, rb_ref, base_ref, e_ref, far_ref, gamma_in, out_ref, held, mt_ref, sems
+def second_gamma_kernel(
+    codes, counts, b_ref, ra_ref, rb_ref, base_ref, e_ref, far_ref, gamma_in, gamma_ref, mt_ref
 ):
     own, far = weights(codes, counts, 3 - first_round(lax.axis_index("mem")))
-    vir, cut = b_ref.shape[0], ra_ref.shape[0]
-    for at, r_ref in ((slice(0, cut), ra_ref), (slice(cut, vir), rb_ref)):
+    cut = ra_ref.shape[0]
+    end = cut + rb_ref.shape[0]
+    for at, r_ref in ((slice(0, cut), ra_ref), (slice(cut, end), rb_ref)):
         mt_ref[:, at] = amp_part(at, b_ref, r_ref, base_ref, e_ref, far_ref)
-
-    def strip(at):
+    aux = gamma_ref.shape[1]
+    for p in range(STRIPS):
+        at = pl.ds(p * (aux // STRIPS), aux // STRIPS)
         total = nn(mt_ref[:, :cut], ra_ref[:, at]) + nn(mt_ref[:, cut:], rb_ref[:, at])
-        return gamma_in[:, at] + (own + far) * total
-
-    strips_out(out_ref, held, sems, strip)
+        gamma_ref[:, at] = gamma_in[:, at] + (own + far) * total
+
+
+def last_gamma_kernel(
+    codes, counts, b_ref, r_ref, base_ref, e_ref, far_ref, gamma_in, out_ref, held, sems
+):
+    own, far = weights(codes, counts, 3 - first_round(lax.axis_index("mem")))
+    vir = b_ref.shape[0]
+    mt = amp_part(slice(vir - r_ref.shape[0], vir), b_ref, r_ref, base_ref, e_ref, far_ref)
+    strips_out(out_ref, held, sems, lambda at: gamma_in[:, at] + (own + far) * nn(mt, r_ref[:, at]))
 
 
 def apply_kernel(mine_ref, other_ref, b_ref, out_ref, tile, held, sems):
@@ -224,25 +233,25 @@
     near = [(0, 3)]
     along = [(0, (1 << k) | 3) for k in range(2, members.bit_length() - 1)]
     across = [(1 << k, 0) for k in range(groups.bit_length() - 1)]
-    for masks in zip(near + across + along, near + along + across):
+    for masks in zip(near + along + across, near + across[1:] + along + across[:1]):
         got = swap(total.astype(BF16), masks)
         total = total + got.astype(F32)
     mine = (total * (1.0 / (8.0 * groups * members))).astype(BF16)
     other = swap(mine, [(0, 1), (0, 1)])
 
     second_energy = turn(occ_energy, True).astype(F32)
-    cut = vir // 4
-    parta, partb = block[:cut], block[cut:]
-    seconda = turn(parta, True)
-    secondb = turn(partb, True)
+    cuts = (0, vir // 4, vir // 2, vir)
+    parts = [block[a:b] for a, b in zip(cuts, cuts[1:])]
+    second = [turn(part, True) for part in parts]
     gamma = call(first_gamma_kernel, wide, (), (0, 1), 5, dot)(
         pair_code, pair_count, gamma, mt, first
     )
+    gamma = call(
+        second_gamma_kernel, wide, [pltpu.VMEM((vir, cuts[2]), BF16)], (0, 1, 6, 7), 9, dot
+    )(pair_code, pair_count, block, second[0], second[1], base, energy, second_energy, gamma)
     result = call(
-        last_gamma_kernel, shape((vir, aux), BF16),
-        [out_scratch[0], pltpu.VMEM((vir, vir), BF16), out_scratch[1]],
-        (0, 1, 6, 7), 9, 2 * dot, any_space,
-    )(pair_code, pair_count, block, seconda, secondb, base, energy, second_energy, gamma)
+        last_gamma_kernel, shape((vir, aux), BF16), out_scratch, (0, 1, 5, 6), 8, dot, any_space
+    )(pair_code, pair_count, block, second[2], base, energy, second_energy, gamma)
     lagrangian = call(
         apply_kernel, shape((vir, aux), BF16), [pltpu.VMEM((vir, vir), BF16), *out_scratch], (), 3, dot,
         any_space,

time: 76 us -> 81.6 us (1.074)
  waiting for transfers between devices: 38 us -> 45.6 us
  starting transfers between devices: 15.5 us -> 12.3 us
  Pallas kernels: 15.6 us -> 16.5 us
    ppermute x5 -> x6, waiting for transfers between devices: 25.9 us -> 32.3 us  [turn(): return lax.ppermute(value, 'mem', pairs)]
    ppermute x5 -> x6, starting transfers between devices: 9.55 us -> 4.19 us  [turn(): return lax.ppermute(value, 'mem', pairs)]
    ppermute x6, starting transfers between devices: 5.94 us -> 8.11 us  [swap(): return lax.ppermute(value, ('grp', 'mem'), pairs)]
    ppermute x6, waiting for transfers between devices: 12.1 us -> 13.3 us  [swap(): return lax.ppermute(value, ('grp', 'mem'), pairs)]
    pallas_call x5 -> x6, Pallas kernels: 15.6 us -> 16.5 us  [call(): kernel_call(kernel, outs, scratch, smem, count, flops, out_spec)(*args)]
    unnamed x9 -> x7, local copies, waits for them, and re-layouts: 3.01 us -> 3.01 us
  transfers between devices with their start and end apart: 11 -> 12, of which waited for: 7 -> 6; matrix products, arithmetic and copies ran while one was open for 2% -> 2% of each run, Pallas kernels for 14% -> 15%
where the time goes in v1:
time: 81.6 us; the launch traced here: 81.4 us
  waiting for transfers between devices  45.6 us (56%)
  Pallas kernels  16.5 us (20%)
  starting transfers between devices  12.3 us (15%)
  local copies, waits for them, and re-layouts  3.14 us (4%)
  between operations  2.83 us (3%)
  other arithmetic  0.99 us (1%)
    ppermute x6, waiting for transfers between devices, turn(): return lax.ppermute(value, 'mem', pairs)  32.3 us
    pallas_call x6, Pallas kernels, call(): kernel_call(kernel, outs, scratch, smem, count, flops, out_spec)(*args)  16.5 us
    ppermute x6, waiting for transfers between devices, swap(): return lax.ppermute(value, ('grp', 'mem'), pairs)  13.3 us
    ppermute x6, starting transfers between devices, swap(): return lax.ppermute(value, ('grp', 'mem'), pairs)  8.11 us
    ppermute x6, starting transfers between devices, turn(): return lax.ppermute(value, 'mem', pairs)  4.19 us
    unnamed x7, local copies, waits for them, and re-layouts  3.01 us
  transfers between devices with their start and end apart: 12, of which 6 were waited for; matrix products, arithmetic and copies ran while one was open for 2% of the time, Pallas kernels for 15%

profile of v1, /device:TPU:0, one launch (start us, length us, event | category | flops | bytes accessed | tf_op | source)
XLA Modules:
  0.0 81.4 jit_solution(3611413207327713985)
XLA Ops:
  0.6 0.6 collective-permute-start.4
  1.2 2.1 %collective-permute-start.5 = (bf16[1]{0:T(256)(128)(2,1)}, bf16[1]{0:T(256)(128)(2,1)}, u32[]{:S(2)}, u32[]{:S(2)}) collective-permute-start(bf16[1]{0:T(256)(128)(2,1)} %param.6), channel_id=1, source_target_pairs={{0,1},{1,3},{2,0},{3,2},{4,5},{5,7},{6,4},{7,6},{8,9},{9,11},{10,8... | collective-permute-start | bytes 14 | tf_op jit(solution)/shard_map/ppermute | solution.py:31
  4.0 0.8 copy.11.codes
  4.7 0.7 reshape.14
  5.4 0.0 copy-start
  5.4 1.6 %copy-done = bf16[1,512,2048]{2,1,0:T(8,128)(2,1)S(1)} copy-done((bf16[1,512,2048]{2,1,0:T(8,128)(2,1)S(1)}, bf16[1,512,2048]{2,1,0:T(8,128)(2,1)}, u32[]{:S(2)}) %copy-start) | copy-done | bytes 2097176
  7.0 0.0 copy-start.2
  7.0 0.7 copy-done.2
  7.6 3.3 %shard_map.68 = (f32[512,512]{1,0:T(8,128)S(1)}, f32[512,512]{1,0:T(8,128)S(1)}, f32[512,2048]{1,0:T(8,128)S(1)}) custom-call(bf16[512,2048]{1,0:T(8,128)(2,1)S(1)} %bitcast.11, f32[1,512]{1,0:T(1,128)S(1)} %bitcast.16, f32[1]{0:T(128)S(6)} %convert_element_type.40.e_ref, s32[1,8,3]{2,1,0:T(8,128)S(1)} %copy.11.codes, s32[1,8]{1,0:T(1,128)S(1)} %copy-done.2), custom_call_target="tpu_custom_call" | custom-call | flops 2147483648 | bytes 1048576 | tf_op jit(solution)/shard_map/pallas_call | solution.py:187
  11.0 17.0 %collective-permute-done.5 = bf16[1]{0:T(256)(128)(2,1)} collective-permute-done((bf16[1]{0:T(256)(128)(2,1)}, bf16[1]{0:T(256)(128)(2,1)}, u32[]{:S(2)}, u32[]{:S(2)}) %collective-permute-start.5) | collective-permute-done | bytes 34 | tf_op jit(solution)/shard_map/ppermute | solution.py:31
  28.7 0.0 collective-permute-done.4.r_ref
  28.7 2.5 %shard_map.69 = (bf16[512,512]{1,0:T(8,128)(2,1)S(1)}, f32[640,128]{1,0:T(8,128)S(1)}, bf16[640,128]{1,0:T(8,128)(2,1)S(1)}) custom-call(bf16[512,2048]{1,0:T(8,128)(2,1)S(1)} %bitcast.12, bf16[512,2048]{1,0:T(8,128)(2,1)S(1)} %collective-permute-done.4.r_ref, f32[512,512]{1,0:T(8,128)S(1)} %get-tuple-element.8.base_ref, f32[1]{0:T(128)S(6)} %convert_element_type.40.e_ref, ...), custom_call_target="tpu_custom_call" | custom-call | flops 1073741824 | bytes 1048576 | tf_op jit(solution)/shard_map/pallas_call | solution.py:187
  31.2 0.1 collective-permute-start.6
  31.3 1.4 %collective-permute-done.6 = bf16[640,128]{1,0:T(8,128)(2,1)S(1)} collective-permute-done((bf16[640,128]{1,0:T(8,128)(2,1)S(1)}, bf16[640,128]{1,0:T(8,128)(2,1)S(1)}, u32[]{:S(2)}, u32[]{:S(2)}) %collective-permute-start.6) | collective-permute-done | bytes 163872 | tf_op jit(solution)/shard_map/ppermute | solution.py:41
  32.7 0.4 collective-permute-start.7
  33.2 5.8 %collective-permute-done.7 = bf16[640,128]{1,0:T(8,128)(2,1)S(1)} collective-permute-done((bf16[640,128]{1,0:T(8,128)(2,1)S(1)}, bf16[640,128]{1,0:T(8,128)(2,1)S(1)}, u32[]{:S(2)}, u32[]{:S(2)}) %collective-permute-start.7) | collective-permute-done | bytes 163872 | tf_op jit(solution)/shard_map/ppermute | solution.py:41
  39.0 0.1 fusion.3
  39.0 2.3 %collective-permute-start.8 = (bf16[640,128]{1,0:T(8,128)(2,1)S(1)}, bf16[640,128]{1,0:T(8,128)(2,1)S(1)}, u32[]{:S(2)}, u32[]{:S(2)}) collective-permute-start(bf16[640,128]{1,0:T(8,128)(2,1)S(1)} %get-tuple-element.14), channel_id=1, source_target_pairs={{0,7},{1,17},{2,18},{3,4},{4,3},{5,21},{6,22},{7,0},{8,15},{9,25},... | collective-permute-start | bytes 491528 | tf_op jit(solution)/shard_map/ppermute | solution.py:41
  41.4 0.1 slice_bitcast_fusion
  41.4 0.1 collective-permute-start
  41.5 4.3 %collective-permute-done.8 = bf16[640,128]{1,0:T(8,128)(2,1)S(1)} collective-permute-done((bf16[640,128]{1,0:T(8,128)(2,1)S(1)}, bf16[640,128]{1,0:T(8,128)(2,1)S(1)}, u32[]{:S(2)}, u32[]{:S(2)}) %collective-permute-start.8) | collective-permute-done | bytes 163872 | tf_op jit(solution)/shard_map/ppermute | solution.py:41
  45.8 2.0 %collective-permute-start.9 = (bf16[640,128]{1,0:T(8,128)(2,1)S(1)}, bf16[640,128]{1,0:T(8,128)(2,1)S(1)}, u32[]{:S(2)}, u32[]{:S(2)}) collective-permute-start(bf16[640,128]{1,0:T(8,128)(2,1)S(1)} %fusion.1), channel_id=1, source_target_pairs={{0,8},{1,6},{2,5},{3,11},{4,12},{5,2},{6,1},{7,15},{8,0},{9,14},{1... | collective-permute-start | bytes 491528 | tf_op jit(solution)/shard_map/ppermute | solution.py:41
  47.8 0.1 slice_bitcast_fusion.1
  47.9 0.1 collective-permute-start.2
  47.9 1.4 %collective-permute-start.3 = (bf16[128,2048]{1,0:T(8,128)(2,1)S(1)}, bf16[128,2048]{1,0:T(8,128)(2,1)S(1)}, u32[]{:S(2)}, u32[]{:S(2)}) collective-permute-start(bf16[128,2048]{1,0:T(8,128)(2,1)S(1)} %get-tuple-element.16), channel_id=1, source_target_pairs={{1,0},{3,1},{0,2},{2,3},{5,4},{7,5},{4,6},{6,7},{9,8},{11,9},{8,10... | collective-permute-start | bytes 1572872 | tf_op jit(solution)/shard_map/ppermute | solution.py:31
  49.3 1.9 %collective-permute-done.9 = bf16[640,128]{1,0:T(8,128)(2,1)S(1)} collective-permute-done((bf16[640,128]{1,0:T(8,128)(2,1)S(1)}, bf16[640,128]{1,0:T(8,128)(2,1)S(1)}, u32[]{:S(2)}, u32[]{:S(2)}) %collective-permute-start.9) | collective-permute-done | bytes 163872 | tf_op jit(solution)/shard_map/ppermute | solution.py:41
  51.2 0.1 fusion.2
  51.2 2.0 %collective-permute-start.10 = (bf16[640,128]{1,0:T(8,128)(2,1)S(1)}, bf16[640,128]{1,0:T(8,128)(2,1)S(1)}, u32[]{:S(2)}, u32[]{:S(2)}) collective-permute-start(bf16[640,128]{1,0:T(8,128)(2,1)S(1)} %fusion.2), channel_id=1, source_target_pairs={{0,16},{1,9},{2,10},{3,19},{4,20},{5,13},{6,14},{7,23},{8,24},{9,1... | collective-permute-start | bytes 491528 | tf_op jit(solution)/shard_map/ppermute | solution.py:41
  53.3 0.0 collective-permute-start.1
  53.3 15.2 %collective-permute-done.1 = bf16[1]{0:T(256)(128)(2,1)} collective-permute-done((bf16[1]{0:T(256)(128)(2,1)}, bf16[1]{0:T(256)(128)(2,1)}, u32[]{:S(2)}, u32[]{:S(2)}) %collective-permute-start.1) | collective-permute-done | bytes 34 | tf_op jit(solution)/shard_map/ppermute | solution.py:31
  69.2 0.0 copy-start.1
  69.2 1.9 %shard_map.70.gamma_in = f32[512,2048]{1,0:T(8,128)S(1)} custom-call(s32[1,8,3]{2,1,0:T(8,128)S(1)} %copy.11.codes, s32[1,8]{1,0:T(1,128)S(1)} %copy-done.2, f32[512,2048]{1,0:T(8,128)S(1)} %get-tuple-element.9.gamma_in, bf16[512,512]{1,0:T(8,128)(2,1)S(1)} %get-tuple-element.11.mt_ref, bf16[512,2048]{1,0:T(8,128)(2,1)S(1)} %collective-permute-done.4.r_ref), custom_call_target="tpu_custom_call" | custom-call | flops 1073741824 | bytes 1048576 | tf_op jit(solution)/shard_map/pallas_call | solution.py:187
  71.1 0.0 collective-permute-done.10
  71.1 0.1 multiply_convert_fusion.mine_ref
  71.2 1.3 %collective-permute-start.11 = (bf16[640,128]{1,0:T(8,128)(2,1)S(1)}, bf16[640,128]{1,0:T(8,128)(2,1)S(1)}, u32[]{:S(2)}, u32[]{:S(2)}) collective-permute-start(bf16[640,128]{1,0:T(8,128)(2,1)S(1)} %multiply_convert_fusion.mine_ref), channel_id=1, source_target_pairs={{0,1},{1,0},{2,3},{3,2},{4,5},{5,4},{6,7},{7,6},{8,9},{9,8},{10,11... | collective-permute-start | bytes 491528 | tf_op jit(solution)/shard_map/ppermute | solution.py:41
  72.5 0.0 collective-permute-done.2.ra_ref
  72.5 0.0 collective-permute-done.3.rb_ref
  72.5 0.0 copy-done.1
  72.5 2.9 %shard_map.71.gamma_in = f32[512,2048]{1,0:T(8,128)S(1)} custom-call(s32[1,8,3]{2,1,0:T(8,128)S(1)} %copy.11.codes, s32[1,8]{1,0:T(1,128)S(1)} %copy-done.2, bf16[512,2048]{1,0:T(8,128)(2,1)S(1)} %bitcast.13, bf16[128,2048]{1,0:T(8,128)(2,1)S(1)} %collective-permute-done.2.ra_ref, bf16[128,2048]{1,0:T(8,128)(2,1)S(1)} %collective-permute-done.3.rb_ref, ...), custom_call_target="tpu_custom_call" | custom-call | flops 1073741824 | bytes 1048576 | tf_op jit(solution)/shard_map/pallas_call | solution.py:187
  75.4 0.0 collective-permute-done.r_ref
  75.5 3.8 %shard_map.72 = bf16[512,2048]{1,0:T(8,128)(2,1)} custom-call(s32[1,8,3]{2,1,0:T(8,128)S(1)} %copy.11.codes, s32[1,8]{1,0:T(1,128)S(1)} %copy-done.2, bf16[512,2048]{1,0:T(8,128)(2,1)S(1)} %bitcast.14, bf16[256,2048]{1,0:T(8,128)(2,1)S(1)} %collective-permute-done.r_ref, f32[512,512]{1,0:T(8,128)S(1)} %get-tuple-element.8.base_ref, ...), custom_call_target="tpu_custom_call" | custom-call | flops 1073741824 | bytes 1048576 | tf_op jit(solution)/shard_map/pallas_call | solution.py:187
  79.2 0.0 collective-permute-done.11.other_ref
  79.3 2.1 %shard_map.73 = bf16[512,2048]{1,0:T(8,128)(2,1)} custom-call(bf16[640,128]{1,0:T(8,128)(2,1)S(1)} %multiply_convert_fusion.mine_ref, bf16[640,128]{1,0:T(8,128)(2,1)S(1)} %collective-permute-done.11.other_ref, bf16[512,2048]{1,0:T(8,128)(2,1)S(1)} %bitcast.15), custom_call_target="tpu_custom_call" | custom-call | flops 1073741824 | bytes 1048576 | tf_op jit(solution)/shard_map/pallas_call | solution.py:187
  (2 shorter events, 0.1 us)
Async XLA Ops:
  0.6 28.1 %collective-permute-start.4 = (bf16[512,2048]{1,0:T(8,128)(2,1)}, bf16[512,2048]{1,0:T(8,128)(2,1)S(1)}, u32[]{:S(2)}, u32[]{:S(2)}) collective-permute-start(bf16[512,2048]{1,0:T(8,128)(2,1)} %bitcast.10), channel_id=1, source_target_pairs={{0,1},{1,3},{2,0},{3,2},{4,5},{5,7},{6,4},{7,6},{8,9},{9,11},{10,8... | collective-permute-start | bytes 6291464 | tf_op jit(solution)/shard_map/ppermute | solution.py:31
  1.2 26.8 %collective-permute-start.5 = (bf16[1]{0:T(256)(128)(2,1)}, bf16[1]{0:T(256)(128)(2,1)}, u32[]{:S(2)}, u32[]{:S(2)}) collective-permute-start(bf16[1]{0:T(256)(128)(2,1)} %param.6), channel_id=1, source_target_pairs={{0,1},{1,3},{2,0},{3,2},{4,5},{5,7},{6,4},{7,6},{8,9},{9,11},{10,8... | collective-permute-start | bytes 14 | tf_op jit(solution)/shard_map/ppermute | solution.py:31
  5.4 1.6 %copy-start = (bf16[1,512,2048]{2,1,0:T(8,128)(2,1)S(1)}, bf16[1,512,2048]{2,1,0:T(8,128)(2,1)}, u32[]{:S(2)}) copy-start(bf16[1,512,2048]{2,1,0:T(8,128)(2,1)} %param.5) | copy-start | bytes 6291460
  7.0 0.7 copy-start.2
  31.2 1.5 %collective-permute-start.6 = (bf16[640,128]{1,0:T(8,128)(2,1)S(1)}, bf16[640,128]{1,0:T(8,128)(2,1)S(1)}, u32[]{:S(2)}, u32[]{:S(2)}) collective-permute-start(bf16[640,128]{1,0:T(8,128)(2,1)S(1)} %get-tuple-element.13), channel_id=1, source_target_pairs={{0,1},{1,0},{2,3},{3,2},{4,5},{5,4},{6,7},{7,6},{8,9},{9,8},{10,11... | collective-permute-start | bytes 491528 | tf_op jit(solution)/shard_map/ppermute | solution.py:41
  32.7 6.2 %collective-permute-start.7 = (bf16[640,128]{1,0:T(8,128)(2,1)S(1)}, bf16[640,128]{1,0:T(8,128)(2,1)S(1)}, u32[]{:S(2)}, u32[]{:S(2)}) collective-permute-start(bf16[640,128]{1,0:T(8,128)(2,1)S(1)} %fusion), channel_id=1, source_target_pairs={{0,3},{1,2},{2,1},{3,0},{4,7},{5,6},{6,5},{7,4},{8,11},{9,10},{10,... | collective-permute-start | bytes 491528 | tf_op jit(solution)/shard_map/ppermute | solution.py:41
  39.0 6.7 %collective-permute-start.8 = (bf16[640,128]{1,0:T(8,128)(2,1)S(1)}, bf16[640,128]{1,0:T(8,128)(2,1)S(1)}, u32[]{:S(2)}, u32[]{:S(2)}) collective-permute-start(bf16[640,128]{1,0:T(8,128)(2,1)S(1)} %get-tuple-element.14), channel_id=1, source_target_pairs={{0,7},{1,17},{2,18},{3,4},{4,3},{5,21},{6,22},{7,0},{8,15},{9,25},... | collective-permute-start | bytes 491528 | tf_op jit(solution)/shard_map/ppermute | solution.py:41
  41.4 34.0 %collective-permute-start = (bf16[256,2048]{1,0:T(8,128)(2,1)S(1)}, bf16[256,2048]{1,0:T(8,128)(2,1)S(1)}, u32[]{:S(2)}, u32[]{:S(2)}) collective-permute-start(bf16[256,2048]{1,0:T(8,128)(2,1)S(1)} %slice_bitcast_fusion), channel_id=1, source_target_pairs={{1,0},{3,1},{0,2},{2,3},{5,4},{7,5},{4,6},{6,7},{9,8},{11,9},{8,10... | collective-permute-start | bytes 3145736 | tf_op jit(solution)/shard_map/ppermute | solution.py:31
  45.8 5.4 %collective-permute-start.9 = (bf16[640,128]{1,0:T(8,128)(2,1)S(1)}, bf16[640,128]{1,0:T(8,128)(2,1)S(1)}, u32[]{:S(2)}, u32[]{:S(2)}) collective-permute-start(bf16[640,128]{1,0:T(8,128)(2,1)S(1)} %fusion.1), channel_id=1, source_target_pairs={{0,8},{1,6},{2,5},{3,11},{4,12},{5,2},{6,1},{7,15},{8,0},{9,14},{1... | collective-permute-start | bytes 491528 | tf_op jit(solution)/shard_map/ppermute | solution.py:41
  47.9 24.6 %collective-permute-start.2 = (bf16[128,2048]{1,0:T(8,128)(2,1)S(1)}, bf16[128,2048]{1,0:T(8,128)(2,1)S(1)}, u32[]{:S(2)}, u32[]{:S(2)}) collective-permute-start(bf16[128,2048]{1,0:T(8,128)(2,1)S(1)} %get-tuple-element.17), channel_id=1, source_target_pairs={{1,0},{3,1},{0,2},{2,3},{5,4},{7,5},{4,6},{6,7},{9,8},{11,9},{8,10... | collective-permute-start | bytes 1572872 | tf_op jit(solution)/shard_map/ppermute | solution.py:31
  47.9 24.5 %collective-permute-start.3 = (bf16[128,2048]{1,0:T(8,128)(2,1)S(1)}, bf16[128,2048]{1,0:T(8,128)(2,1)S(1)}, u32[]{:S(2)}, u32[]{:S(2)}) collective-permute-start(bf16[128,2048]{1,0:T(8,128)(2,1)S(1)} %get-tuple-element.16), channel_id=1, source_target_pairs={{1,0},{3,1},{0,2},{2,3},{5,4},{7,5},{4,6},{6,7},{9,8},{11,9},{8,10... | collective-permute-start | bytes 1572872 | tf_op jit(solution)/shard_map/ppermute | solution.py:31
  51.2 19.8 %collective-permute-start.10 = (bf16[640,128]{1,0:T(8,128)(2,1)S(1)}, bf16[640,128]{1,0:T(8,128)(2,1)S(1)}, u32[]{:S(2)}, u32[]{:S(2)}) collective-permute-start(bf16[640,128]{1,0:T(8,128)(2,1)S(1)} %fusion.2), channel_id=1, source_target_pairs={{0,16},{1,9},{2,10},{3,19},{4,20},{5,13},{6,14},{7,23},{8,24},{9,1... | collective-permute-start | bytes 491528 | tf_op jit(solution)/shard_map/ppermute | solution.py:41
  53.3 15.2 %collective-permute-start.1 = (bf16[1]{0:T(256)(128)(2,1)}, bf16[1]{0:T(256)(128)(2,1)}, u32[]{:S(2)}, u32[]{:S(2)}) collective-permute-start(bf16[1]{0:T(256)(128)(2,1)} %param.6), channel_id=1, source_target_pairs={{1,0},{3,1},{0,2},{2,3},{5,4},{7,5},{4,6},{6,7},{9,8},{11,9},{8,10... | collective-permute-start | bytes 14 | tf_op jit(solution)/shard_map/ppermute | solution.py:31
  69.2 3.3 %copy-start.1 = (bf16[1,512,2048]{2,1,0:T(8,128)(2,1)S(1)}, bf16[1,512,2048]{2,1,0:T(8,128)(2,1)}, u32[]{:S(2)}) copy-start(bf16[1,512,2048]{2,1,0:T(8,128)(2,1)} %param.5) | copy-start | bytes 6291460
  71.2 8.0 %collective-permute-start.11 = (bf16[640,128]{1,0:T(8,128)(2,1)S(1)}, bf16[640,128]{1,0:T(8,128)(2,1)S(1)}, u32[]{:S(2)}, u32[]{:S(2)}) collective-permute-start(bf16[640,128]{1,0:T(8,128)(2,1)S(1)} %multiply_convert_fusion.mine_ref), channel_id=1, source_target_pairs={{0,1},{1,0},{2,3},{3,2},{4,5},{5,4},{6,7},{7,6},{8,9},{9,8},{10,11... | collective-permute-start | bytes 491528 | tf_op jit(solution)/shard_map/ppermute | solution.py:41

commit v2 on v1

--- a/solution.py
+++ b/solution.py
@@ -65,17 +65,19 @@
     return jnp.dot(a, b, preferred_element_type=F32)
 
 
-def early_kernel(b_ref, row_ref, e_ref, codes, counts, base_ref, dens_ref, gamma_ref, amp):
+def early_kernel(
+    b_ref, row_ref, e_ref, first_ref, second_ref, codes, counts, one_ref, two_ref, dens_ref, gamma_ref, amp
+):
     vir, aux = b_ref.shape
     row = row_ref[...]
-    col = jnp.broadcast_to(row, (vir, vir)).T
-    base_ref[...] = col + row
+    sums = jnp.broadcast_to(row, (vir, vir)).T + row - e_ref[0]
+    one_ref[...] = 1.0 / (sums - first_ref[0])
+    two_ref[...] = 1.0 / (sums - second_ref[0])
     own, _ = weights(codes, counts, 0)
-    energy = e_ref[0]
     half = vir // 2
     for at in (slice(0, half), slice(half, vir)):
         k = nt(b_ref[...], b_ref[at, :])
-        amp[:, at] = (k / (base_ref[:, at] - energy - energy)).astype(BF16)
+        amp[:, at] = (k / (sums[:, at] - e_ref[0])).astype(BF16)
     a = amp[...]
     dens_ref[...] = own * nn(a, a)
     for p in range(STRIPS):
@@ -83,9 +85,8 @@
         gamma_ref[:, at] = (2.0 * own) * nn(a, b_ref[:, at])
 
 
-def amp_part(at, b_ref, r_ref, base_ref, e_ref, far_ref):
-    k = nt(b_ref[...], r_ref[...])
-    return (k / (base_ref[:, at] - e_ref[0] - far_ref[0])).astype(BF16)
+def amp_part(at, b_ref, r_ref, over_ref):
+    return (nt(b_ref[...], r_ref[...]) * over_ref[:, at]).astype(BF16)
 
 
 def blocks(size):
@@ -93,13 +94,13 @@
     return [(i, j) for i in range(count) for j in range(i, count)]
 
 
-def density_kernel(b_ref, r_ref, base_ref, e_ref, far_ref, codes, counts, dens_in, mt_ref, keep_ref, send_ref, m_ref):
+def density_kernel(b_ref, r_ref, over_ref, codes, counts, dens_in, mt_ref, keep_ref, send_ref, m_ref):
     vir = b_ref.shape[0]
     half = vir // 2
     me = lax.axis_index("mem")
     own, far = weights(codes, counts, first_round(me))
     for at in (slice(0, half), slice(half, vir)):
-        mt = amp_part(at, b_ref, r_ref.at[at, :], base_ref, e_ref, far_ref)
+        mt = amp_part(at, b_ref, r_ref.at[at, :], over_ref)
         mt_ref[:, at] = mt
         m_ref[at, :] = mt.T
     high, low = slice(0, half), slice(half, vir)
@@ -133,10 +134,10 @@
         gamma_ref[:, at] = gamma_in[:, at] + (own + far) * nn(mt_ref[...], r_ref[:, at])
 
 
-def strips_out(out_ref, held, sems, compute):
-    step = held.shape[1] // STRIPS
+def strips_out(out_ref, held, sems, strips, compute):
+    step = held.shape[1] // strips
     copies = []
-    for p in range(STRIPS):
+    for p in range(strips):
         at = pl.ds(p * step, step)
         held[:, at] = compute(at).astype(held.dtype)
         copies.append(pltpu.make_async_copy(held.at[:, at], out_ref.at[:, at], sems.at[p]))
@@ -145,28 +146,25 @@
         copy.wait()
 
 
-def second_gamma_kernel(
-    codes, counts, b_ref, ra_ref, rb_ref, base_ref, e_ref, far_ref, gamma_in, gamma_ref, mt_ref
-):
+def second_gamma_kernel(codes, counts, b_ref, over_ref, gamma_in, *refs):
+    parts, (gamma_ref, held) = refs[:-2], refs[-2:]
     own, far = weights(codes, counts, 3 - first_round(lax.axis_index("mem")))
-    cut = ra_ref.shape[0]
-    end = cut + rb_ref.shape[0]
-    for at, r_ref in ((slice(0, cut), ra_ref), (slice(cut, end), rb_ref)):
-        mt_ref[:, at] = amp_part(at, b_ref, r_ref, base_ref, e_ref, far_ref)
+    start = 0
+    for part in parts:
+        held[start : start + part.shape[0], :] = part[...]
+        start += part.shape[0]
+    mt = amp_part(slice(0, start), b_ref, held, over_ref)
     aux = gamma_ref.shape[1]
     for p in range(STRIPS):
         at = pl.ds(p * (aux // STRIPS), aux // STRIPS)
-        total = nn(mt_ref[:, :cut], ra_ref[:, at]) + nn(mt_ref[:, cut:], rb_ref[:, at])
-        gamma_ref[:, at] = gamma_in[:, at] + (own + far) * total
-
-
-def last_gamma_kernel(
-    codes, counts, b_ref, r_ref, base_ref, e_ref, far_ref, gamma_in, out_ref, held, sems
-):
+        gamma_ref[:, at] = gamma_in[:, at] + (own + far) * nn(mt, held[:, at])
+
+
+def last_gamma_kernel(codes, counts, b_ref, over_ref, gamma_in, r_ref, out_ref, held, sems):
     own, far = weights(codes, counts, 3 - first_round(lax.axis_index("mem")))
     vir = b_ref.shape[0]
-    mt = amp_part(slice(vir - r_ref.shape[0], vir), b_ref, r_ref, base_ref, e_ref, far_ref)
-    strips_out(out_ref, held, sems, lambda at: gamma_in[:, at] + (own + far) * nn(mt, r_ref[:, at]))
+    mt = amp_part(slice(vir - r_ref.shape[0], vir), b_ref, r_ref, over_ref)
+    strips_out(out_ref, held, sems, 2, lambda at: gamma_in[:, at] + (own + far) * nn(mt, r_ref[:, at]))
 
 
 def apply_kernel(mine_ref, other_ref, b_ref, out_ref, tile, held, sems):
@@ -180,7 +178,7 @@
         tile[pl.ds(i * TILE, TILE), pl.ds(j * TILE, TILE)] = block
         if i != j:
             tile[pl.ds(j * TILE, TILE), pl.ds(i * TILE, TILE)] = block.T
-    strips_out(out_ref, held, sems, lambda at: nn(tile[...], b_ref[:, at]))
+    strips_out(out_ref, held, sems, STRIPS, lambda at: nn(tile[...], b_ref[:, at]))
 
 
 def call(kernel, outs, scratch=(), smem=(), count=0, flops=0, out_spec=VMEM):
@@ -215,19 +213,21 @@
 
     first_energy = turn(occ_energy, False).astype(F32)
     first = turn(block, False)
+    second_energy = turn(occ_energy, True).astype(F32)
 
     energy = occ_energy.astype(F32)
     row = vir_energy.astype(F32).reshape(1, vir)
-    base, dens, gamma = call(
-        early_kernel, (square, square, wide), [pltpu.VMEM((vir, vir), BF16)], (2, 3, 4), 5, 2 * dot
-    )(block, row, energy, pair_code, pair_count)
+    over_first, over_second, dens, gamma = call(
+        early_kernel, (square, square, square, wide), [pltpu.VMEM((vir, vir), BF16)],
+        (2, 3, 4, 5, 6), 7, 2 * dot,
+    )(block, row, energy, first_energy, second_energy, pair_code, pair_count)
 
     half = len(blocks(vir)) * TILE // 2
     mt, keep, send = call(
         density_kernel,
         (shape((vir, vir), BF16), shape((half, TILE), F32), shape((half, TILE), BF16)),
-        [pltpu.VMEM((vir, vir), BF16)], (3, 4, 5, 6), 8, dot,
-    )(block, first, base, energy, first_energy, pair_code, pair_count, dens)
+        [pltpu.VMEM((vir, vir), BF16)], (3, 4), 6, dot,
+    )(block, first, over_first, pair_code, pair_count, dens)
 
     total = keep + swap(send, [(0, 1), (0, 1)]).astype(F32)
     near = [(0, 3)]
@@ -239,19 +239,19 @@
     mine = (total * (1.0 / (8.0 * groups * members))).astype(BF16)
     other = swap(mine, [(0, 1), (0, 1)])
 
-    second_energy = turn(occ_energy, True).astype(F32)
-    cuts = (0, vir // 4, vir // 2, vir)
+    unit = vir // 32
+    cuts = (0, 7 * unit, 13 * unit, 16 * unit, vir)
     parts = [block[a:b] for a, b in zip(cuts, cuts[1:])]
     second = [turn(part, True) for part in parts]
     gamma = call(first_gamma_kernel, wide, (), (0, 1), 5, dot)(
         pair_code, pair_count, gamma, mt, first
     )
     gamma = call(
-        second_gamma_kernel, wide, [pltpu.VMEM((vir, cuts[2]), BF16)], (0, 1, 6, 7), 9, dot
-    )(pair_code, pair_count, block, second[0], second[1], base, energy, second_energy, gamma)
+        second_gamma_kernel, wide, [pltpu.VMEM((cuts[3], aux), BF16)], (0, 1), 8, dot
+    )(pair_code, pair_count, block, over_second, gamma, *second[:3])
     result = call(
-        last_gamma_kernel, shape((vir, aux), BF16), out_scratch, (0, 1, 5, 6), 8, dot, any_space
-    )(pair_code, pair_count, block, second[2], base, energy, second_energy, gamma)
+        last_gamma_kernel, shape((vir, aux), BF16), out_scratch, (0, 1), 6, dot, any_space
+    )(pair_code, pair_count, block, over_second, gamma, second[3])
     lagrangian = call(
         apply_kernel, shape((vir, aux), BF16), [pltpu.VMEM((vir, vir), BF16), *out_scratch], (), 3, dot,
         any_space,

time: 81.6 us -> 80.4 us (0.985)
  starting transfers between devices: 12.3 us -> 11 us
    ppermute x6 -> x7, waiting for transfers between devices: 32.3 us -> 27.1 us  [turn(): return lax.ppermute(value, 'mem', pairs)]
    ppermute x6, waiting for transfers between devices: 13.3 us -> 18.3 us  [swap(): return lax.ppermute(value, ('grp', 'mem'), pairs)]
    ppermute x6, starting transfers between devices: 8.11 us -> 6.04 us  [swap(): return lax.ppermute(value, ('grp', 'mem'), pairs)]
    ppermute x6 -> x7, starting transfers between devices: 4.19 us -> 4.92 us  [turn(): return lax.ppermute(value, 'mem', pairs)]
  transfers between devices with their start and end apart: 12 -> 13, of which waited for: 6 -> 7; matrix products, arithmetic and copies ran while one was open for 2% -> 2% of each run, Pallas kernels for 15% -> 15%
where the time goes in v2:
time: 80.4 us; the launch traced here: 80.2 us
  waiting for transfers between devices  45.4 us (56%)
  Pallas kernels  16.9 us (21%)
  starting transfers between devices  11 us (14%)
  local copies, waits for them, and re-layouts  3.14 us (4%)
  between operations  2.88 us (4%)
  other arithmetic  0.96 us (1%)
    ppermute x7, waiting for transfers between devices, turn(): return lax.ppermute(value, 'mem', pairs)  27.1 us
    ppermute x6, waiting for transfers between devices, swap(): return lax.ppermute(value, ('grp', 'mem'), pairs)  18.3 us
    pallas_call x6, Pallas kernels, call(): kernel_call(kernel, outs, scratch, smem, count, flops, out_spec)(*args)  16.9 us
    ppermute x6, starting transfers between devices, swap(): return lax.ppermute(value, ('grp', 'mem'), pairs)  6.04 us
    ppermute x7, starting transfers between devices, turn(): return lax.ppermute(value, 'mem', pairs)  4.92 us
    unnamed x7, local copies, waits for them, and re-layouts  3 us
  transfers between devices with their start and end apart: 13, of which 7 were waited for; matrix products, arithmetic and copies ran while one was open for 2% of the time, Pallas kernels for 15%

profile of v2, /device:TPU:0, one launch (start us, length us, event | category | flops | bytes accessed | tf_op | source)
XLA Modules:
  0.0 80.2 jit_solution(5836214378595032546)
XLA Ops:
  0.6 0.6 collective-permute-start.2
  1.2 2.1 %collective-permute-start = (bf16[1]{0:T(256)(128)(2,1)}, bf16[1]{0:T(256)(128)(2,1)}, u32[]{:S(2)}, u32[]{:S(2)}) collective-permute-start(bf16[1]{0:T(256)(128)(2,1)} %param.6), channel_id=1, source_target_pairs={{0,1},{1,3},{2,0},{3,2},{4,5},{5,7},{6,4},{7,6},{8,9},{9,11},{10,8... | collective-permute-start | bytes 14 | tf_op jit(solution)/shard_map/ppermute | solution.py:31
  3.3 0.6 collective-permute-start.1
  4.6 0.8 copy.11.codes
  5.3 0.7 reshape.15
  6.0 22.0 %collective-permute-done = bf16[1]{0:T(256)(128)(2,1)} collective-permute-done((bf16[1]{0:T(256)(128)(2,1)}, bf16[1]{0:T(256)(128)(2,1)}, u32[]{:S(2)}, u32[]{:S(2)}) %collective-permute-start) | collective-permute-done | bytes 34 | tf_op jit(solution)/shard_map/ppermute | solution.py:31
  28.7 0.0 collective-permute-done.1
  29.4 0.0 copy-start
  29.4 1.6 %copy-done = bf16[1,512,2048]{2,1,0:T(8,128)(2,1)S(1)} copy-done((bf16[1,512,2048]{2,1,0:T(8,128)(2,1)S(1)}, bf16[1,512,2048]{2,1,0:T(8,128)(2,1)}, u32[]{:S(2)}) %copy-start) | copy-done | bytes 2097176
  31.0 0.0 copy-start.2
  31.0 0.7 copy-done.2
  31.7 3.5 %shard_map.68 = (f32[512,512]{1,0:T(8,128)S(1)}, f32[512,512]{1,0:T(8,128)S(1)}, f32[512,512]{1,0:T(8,128)S(1)}, f32[512,2048]{1,0:T(8,128)S(1)}) custom-call(bf16[512,2048]{1,0:T(8,128)(2,1)S(1)} %bitcast.13, f32[1,512]{1,0:T(1,128)S(1)} %bitcast.18, f32[1]{0:T(128)S(6)} %convert_element_type.40.e_ref, f32[1]{0:T(128)S(6)} %convert_element_type.41.first_ref, ...), custom_call_target="tpu_custom_call" | custom-call | flops 2147483648 | bytes 1048576 | tf_op jit(solution)/shard_map/pallas_call | solution.py:185
  35.2 0.0 collective-permute-done.2.r_ref
  35.2 2.5 %shard_map.69 = (bf16[512,512]{1,0:T(8,128)(2,1)S(1)}, f32[640,128]{1,0:T(8,128)S(1)}, bf16[640,128]{1,0:T(8,128)(2,1)S(1)}) custom-call(bf16[512,2048]{1,0:T(8,128)(2,1)S(1)} %bitcast.14, bf16[512,2048]{1,0:T(8,128)(2,1)S(1)} %collective-permute-done.2.r_ref, f32[512,512]{1,0:T(8,128)S(1)} %get-tuple-element.11.over_ref, s32[1,8,3]{2,1,0:T(8,128)S(1)} %copy.11.codes, ...), custom_call_target="tpu_custom_call" | custom-call | flops 1073741824 | bytes 1048576 | tf_op jit(solution)/shard_map/pallas_call | solution.py:185
  37.7 0.1 collective-permute-start.7
  37.7 1.4 %collective-permute-done.7 = bf16[640,128]{1,0:T(8,128)(2,1)S(1)} collective-permute-done((bf16[640,128]{1,0:T(8,128)(2,1)S(1)}, bf16[640,128]{1,0:T(8,128)(2,1)S(1)}, u32[]{:S(2)}, u32[]{:S(2)}) %collective-permute-start.7) | collective-permute-done | bytes 163872 | tf_op jit(solution)/shard_map/ppermute | solution.py:41
  39.2 0.4 collective-permute-start.8
  39.6 1.5 %collective-permute-start.3 = (bf16[112,2048]{1,0:T(8,128)(2,1)S(1)}, bf16[112,2048]{1,0:T(8,128)(2,1)S(1)}, u32[]{:S(2)}, u32[]{:S(2)}) collective-permute-start(bf16[112,2048]{1,0:T(8,128)(2,1)S(1)} %slice_bitcast_fusion.1), channel_id=1, source_target_pairs={{1,0},{3,1},{0,2},{2,3},{5,4},{7,5},{4,6},{6,7},{9,8},{11,9},{8,10... | collective-permute-start | bytes 1376264 | tf_op jit(solution)/shard_map/ppermute | solution.py:31
  41.1 4.3 %collective-permute-done.8 = bf16[640,128]{1,0:T(8,128)(2,1)S(1)} collective-permute-done((bf16[640,128]{1,0:T(8,128)(2,1)S(1)}, bf16[640,128]{1,0:T(8,128)(2,1)S(1)}, u32[]{:S(2)}, u32[]{:S(2)}) %collective-permute-start.8) | collective-permute-done | bytes 163872 | tf_op jit(solution)/shard_map/ppermute | solution.py:41
  45.4 0.1 fusion.3
  45.5 2.3 %collective-permute-start.9 = (bf16[640,128]{1,0:T(8,128)(2,1)S(1)}, bf16[640,128]{1,0:T(8,128)(2,1)S(1)}, u32[]{:S(2)}, u32[]{:S(2)}) collective-permute-start(bf16[640,128]{1,0:T(8,128)(2,1)S(1)} %get-tuple-element.16), channel_id=1, source_target_pairs={{0,7},{1,17},{2,18},{3,4},{4,3},{5,21},{6,22},{7,0},{8,15},{9,25},... | collective-permute-start | bytes 491528 | tf_op jit(solution)/shard_map/ppermute | solution.py:41
  47.8 0.1 collective-permute-start.4
  47.9 7.1 %collective-permute-done.9 = bf16[640,128]{1,0:T(8,128)(2,1)S(1)} collective-permute-done((bf16[640,128]{1,0:T(8,128)(2,1)S(1)}, bf16[640,128]{1,0:T(8,128)(2,1)S(1)}, u32[]{:S(2)}, u32[]{:S(2)}) %collective-permute-start.9) | collective-permute-done | bytes 163872 | tf_op jit(solution)/shard_map/ppermute | solution.py:41
  55.0 1.6 %collective-permute-start.10 = (bf16[640,128]{1,0:T(8,128)(2,1)S(1)}, bf16[640,128]{1,0:T(8,128)(2,1)S(1)}, u32[]{:S(2)}, u32[]{:S(2)}) collective-permute-start(bf16[640,128]{1,0:T(8,128)(2,1)S(1)} %fusion.1), channel_id=1, source_target_pairs={{0,8},{1,6},{2,5},{3,11},{4,12},{5,2},{6,1},{7,15},{8,0},{9,14},{1... | collective-permute-start | bytes 491528 | tf_op jit(solution)/shard_map/ppermute | solution.py:41
  56.6 0.1 slice_bitcast_fusion
  56.6 0.1 collective-permute-start.6
  56.7 3.7 %collective-permute-done.10 = bf16[640,128]{1,0:T(8,128)(2,1)S(1)} collective-permute-done((bf16[640,128]{1,0:T(8,128)(2,1)S(1)}, bf16[640,128]{1,0:T(8,128)(2,1)S(1)}, u32[]{:S(2)}, u32[]{:S(2)}) %collective-permute-start.10) | collective-permute-done | bytes 163872 | tf_op jit(solution)/shard_map/ppermute | solution.py:41
  60.4 0.1 fusion.2
  60.5 1.6 %collective-permute-start.11 = (bf16[640,128]{1,0:T(8,128)(2,1)S(1)}, bf16[640,128]{1,0:T(8,128)(2,1)S(1)}, u32[]{:S(2)}, u32[]{:S(2)}) collective-permute-start(bf16[640,128]{1,0:T(8,128)(2,1)S(1)} %fusion.2), channel_id=1, source_target_pairs={{0,16},{1,9},{2,10},{3,19},{4,20},{5,13},{6,14},{7,23},{8,24},{9,1... | collective-permute-start | bytes 491528 | tf_op jit(solution)/shard_map/ppermute | solution.py:41
  62.1 0.1 collective-permute-start.5
  62.1 0.0 copy-start.1
  62.1 1.9 %shard_map.70.gamma_in = f32[512,2048]{1,0:T(8,128)S(1)} custom-call(s32[1,8,3]{2,1,0:T(8,128)S(1)} %copy.11.codes, s32[1,8]{1,0:T(1,128)S(1)} %copy-done.2, f32[512,2048]{1,0:T(8,128)S(1)} %get-tuple-element.10.gamma_in, bf16[512,512]{1,0:T(8,128)(2,1)S(1)} %get-tuple-element.13.mt_ref, bf16[512,2048]{1,0:T(8,128)(2,1)S(1)} %collective-permute-done.2.r_ref), custom_call_target="tpu_custom_call" | custom-call | flops 1073741824 | bytes 1048576 | tf_op jit(solution)/shard_map/pallas_call | solution.py:185
  64.0 1.8 %collective-permute-done.11 = bf16[640,128]{1,0:T(8,128)(2,1)S(1)} collective-permute-done((bf16[640,128]{1,0:T(8,128)(2,1)S(1)}, bf16[640,128]{1,0:T(8,128)(2,1)S(1)}, u32[]{:S(2)}, u32[]{:S(2)}) %collective-permute-start.11) | collective-permute-done | bytes 163872 | tf_op jit(solution)/shard_map/ppermute | solution.py:41
  65.8 0.1 multiply_convert_fusion.mine_ref
  65.9 0.1 collective-permute-start.12
  66.0 5.1 %collective-permute-done.5.refs_2_ = bf16[48,2048]{1,0:T(8,128)(2,1)S(1)} collective-permute-done((bf16[48,2048]{1,0:T(8,128)(2,1)S(1)}, bf16[48,2048]{1,0:T(8,128)(2,1)S(1)}, u32[]{:S(2)}, u32[]{:S(2)}) %collective-permute-start.5) | collective-permute-done | bytes 196640 | tf_op jit(solution)/shard_map/ppermute | solution.py:31
  71.1 0.0 collective-permute-done.4.refs_1_
  71.1 0.0 collective-permute-done.3.refs_0_
  71.1 0.0 copy-done.1
  71.1 3.0 %shard_map.71.gamma_in = f32[512,2048]{1,0:T(8,128)S(1)} custom-call(s32[1,8,3]{2,1,0:T(8,128)S(1)} %copy.11.codes, s32[1,8]{1,0:T(1,128)S(1)} %copy-done.2, bf16[512,2048]{1,0:T(8,128)(2,1)S(1)} %bitcast.15, f32[512,512]{1,0:T(8,128)S(1)} %get-tuple-element.9.over_ref, f32[512,2048]{1,0:T(8,128)S(1)} %shard_map.70.gamma_in, ...), custom_call_target="tpu_custom_call" | custom-call | flops 1073741824 | bytes 1048576 | tf_op jit(solution)/shard_map/pallas_call | solution.py:185
  74.1 0.0 collective-permute-done.6.r_ref
  74.1 4.0 %shard_map.72 = bf16[512,2048]{1,0:T(8,128)(2,1)} custom-call(s32[1,8,3]{2,1,0:T(8,128)S(1)} %copy.11.codes, s32[1,8]{1,0:T(1,128)S(1)} %copy-done.2, bf16[512,2048]{1,0:T(8,128)(2,1)S(1)} %bitcast.16, f32[512,512]{1,0:T(8,128)S(1)} %get-tuple-element.9.over_ref, f32[512,2048]{1,0:T(8,128)S(1)} %shard_map.71.gamma_in, ...), custom_call_target="tpu_custom_call" | custom-call | flops 1073741824 | bytes 1048576 | tf_op jit(solution)/shard_map/pallas_call | solution.py:185
  78.1 0.0 collective-permute-done.12.other_ref
  78.1 2.1 %shard_map.73 = bf16[512,2048]{1,0:T(8,128)(2,1)} custom-call(bf16[640,128]{1,0:T(8,128)(2,1)S(1)} %multiply_convert_fusion.mine_ref, bf16[640,128]{1,0:T(8,128)(2,1)S(1)} %collective-permute-done.12.other_ref, bf16[512,2048]{1,0:T(8,128)(2,1)S(1)} %bitcast.17), custom_call_target="tpu_custom_call" | custom-call | flops 1073741824 | bytes 1048576 | tf_op jit(solution)/shard_map/pallas_call | solution.py:185
  (5 shorter events, 0.1 us)
Async XLA Ops:
  0.6 34.5 %collective-permute-start.2 = (bf16[512,2048]{1,0:T(8,128)(2,1)}, bf16[512,2048]{1,0:T(8,128)(2,1)S(1)}, u32[]{:S(2)}, u32[]{:S(2)}) collective-permute-start(bf16[512,2048]{1,0:T(8,128)(2,1)} %bitcast.12), channel_id=1, source_target_pairs={{0,1},{1,3},{2,0},{3,2},{4,5},{5,7},{6,4},{7,6},{8,9},{9,11},{10,8... | collective-permute-start | bytes 6291464 | tf_op jit(solution)/shard_map/ppermute | solution.py:31
  1.2 26.8 %collective-permute-start = (bf16[1]{0:T(256)(128)(2,1)}, bf16[1]{0:T(256)(128)(2,1)}, u32[]{:S(2)}, u32[]{:S(2)}) collective-permute-start(bf16[1]{0:T(256)(128)(2,1)} %param.6), channel_id=1, source_target_pairs={{0,1},{1,3},{2,0},{3,2},{4,5},{5,7},{6,4},{7,6},{8,9},{9,11},{10,8... | collective-permute-start | bytes 14 | tf_op jit(solution)/shard_map/ppermute | solution.py:31
  3.3 25.4 %collective-permute-start.1 = (bf16[1]{0:T(256)(128)(2,1)}, bf16[1]{0:T(256)(128)(2,1)}, u32[]{:S(2)}, u32[]{:S(2)}) collective-permute-start(bf16[1]{0:T(256)(128)(2,1)} %param.6), channel_id=1, source_target_pairs={{1,0},{3,1},{0,2},{2,3},{5,4},{7,5},{4,6},{6,7},{9,8},{11,9},{8,10... | collective-permute-start | bytes 14 | tf_op jit(solution)/shard_map/ppermute | solution.py:31
  29.4 1.6 %copy-start = (bf16[1,512,2048]{2,1,0:T(8,128)(2,1)S(1)}, bf16[1,512,2048]{2,1,0:T(8,128)(2,1)}, u32[]{:S(2)}) copy-start(bf16[1,512,2048]{2,1,0:T(8,128)(2,1)} %param.5) | copy-start | bytes 6291460
  31.0 0.7 copy-start.2
  37.7 1.5 %collective-permute-start.7 = (bf16[640,128]{1,0:T(8,128)(2,1)S(1)}, bf16[640,128]{1,0:T(8,128)(2,1)S(1)}, u32[]{:S(2)}, u32[]{:S(2)}) collective-permute-start(bf16[640,128]{1,0:T(8,128)(2,1)S(1)} %get-tuple-element.15), channel_id=1, source_target_pairs={{0,1},{1,0},{2,3},{3,2},{4,5},{5,4},{6,7},{7,6},{8,9},{9,8},{10,11... | collective-permute-start | bytes 491528 | tf_op jit(solution)/shard_map/ppermute | solution.py:41
  39.2 6.2 %collective-permute-start.8 = (bf16[640,128]{1,0:T(8,128)(2,1)S(1)}, bf16[640,128]{1,0:T(8,128)(2,1)S(1)}, u32[]{:S(2)}, u32[]{:S(2)}) collective-permute-start(bf16[640,128]{1,0:T(8,128)(2,1)S(1)} %fusion), channel_id=1, source_target_pairs={{0,3},{1,2},{2,1},{3,0},{4,7},{5,6},{6,5},{7,4},{8,11},{9,10},{10,... | collective-permute-start | bytes 491528 | tf_op jit(solution)/shard_map/ppermute | solution.py:41
  39.6 31.5 %collective-permute-start.3 = (bf16[112,2048]{1,0:T(8,128)(2,1)S(1)}, bf16[112,2048]{1,0:T(8,128)(2,1)S(1)}, u32[]{:S(2)}, u32[]{:S(2)}) collective-permute-start(bf16[112,2048]{1,0:T(8,128)(2,1)S(1)} %slice_bitcast_fusion.1), channel_id=1, source_target_pairs={{1,0},{3,1},{0,2},{2,3},{5,4},{7,5},{4,6},{6,7},{9,8},{11,9},{8,10... | collective-permute-start | bytes 1376264 | tf_op jit(solution)/shard_map/ppermute | solution.py:31
  45.5 9.5 %collective-permute-start.9 = (bf16[640,128]{1,0:T(8,128)(2,1)S(1)}, bf16[640,128]{1,0:T(8,128)(2,1)S(1)}, u32[]{:S(2)}, u32[]{:S(2)}) collective-permute-start(bf16[640,128]{1,0:T(8,128)(2,1)S(1)} %get-tuple-element.16), channel_id=1, source_target_pairs={{0,7},{1,17},{2,18},{3,4},{4,3},{5,21},{6,22},{7,0},{8,15},{9,25},... | collective-permute-start | bytes 491528 | tf_op jit(solution)/shard_map/ppermute | solution.py:41
  47.8 23.3 %collective-permute-start.4 = (bf16[96,2048]{1,0:T(8,128)(2,1)S(1)}, bf16[96,2048]{1,0:T(8,128)(2,1)S(1)}, u32[]{:S(2)}, u32[]{:S(2)}) collective-permute-start(bf16[96,2048]{1,0:T(8,128)(2,1)S(1)} %slice_bitcast_fusion.2), channel_id=1, source_target_pairs={{1,0},{3,1},{0,2},{2,3},{5,4},{7,5},{4,6},{6,7},{9,8},{11,9},{8,10... | collective-permute-start | bytes 1179656 | tf_op jit(solution)/shard_map/ppermute | solution.py:31
  55.0 5.4 %collective-permute-start.10 = (bf16[640,128]{1,0:T(8,128)(2,1)S(1)}, bf16[640,128]{1,0:T(8,128)(2,1)S(1)}, u32[]{:S(2)}, u32[]{:S(2)}) collective-permute-start(bf16[640,128]{1,0:T(8,128)(2,1)S(1)} %fusion.1), channel_id=1, source_target_pairs={{0,8},{1,6},{2,5},{3,11},{4,12},{5,2},{6,1},{7,15},{8,0},{9,14},{1... | collective-permute-start | bytes 491528 | tf_op jit(solution)/shard_map/ppermute | solution.py:41
  56.6 17.5 %collective-permute-start.6 = (bf16[256,2048]{1,0:T(8,128)(2,1)S(1)}, bf16[256,2048]{1,0:T(8,128)(2,1)S(1)}, u32[]{:S(2)}, u32[]{:S(2)}) collective-permute-start(bf16[256,2048]{1,0:T(8,128)(2,1)S(1)} %slice_bitcast_fusion), channel_id=1, source_target_pairs={{1,0},{3,1},{0,2},{2,3},{5,4},{7,5},{4,6},{6,7},{9,8},{11,9},{8,10... | collective-permute-start | bytes 3145736 | tf_op jit(solution)/shard_map/ppermute | solution.py:31
  60.5 5.4 %collective-permute-start.11 = (bf16[640,128]{1,0:T(8,128)(2,1)S(1)}, bf16[640,128]{1,0:T(8,128)(2,1)S(1)}, u32[]{:S(2)}, u32[]{:S(2)}) collective-permute-start(bf16[640,128]{1,0:T(8,128)(2,1)S(1)} %fusion.2), channel_id=1, source_target_pairs={{0,16},{1,9},{2,10},{3,19},{4,20},{5,13},{6,14},{7,23},{8,24},{9,1... | collective-permute-start | bytes 491528 | tf_op jit(solution)/shard_map/ppermute | solution.py:41
  62.1 9.1 %collective-permute-start.5 = (bf16[48,2048]{1,0:T(8,128)(2,1)S(1)}, bf16[48,2048]{1,0:T(8,128)(2,1)S(1)}, u32[]{:S(2)}, u32[]{:S(2)}) collective-permute-start(bf16[48,2048]{1,0:T(8,128)(2,1)S(1)} %slice_bitcast_fusion.3), channel_id=1, source_target_pairs={{1,0},{3,1},{0,2},{2,3},{5,4},{7,5},{4,6},{6,7},{9,8},{11,9},{8,10... | collective-permute-start | bytes 589832 | tf_op jit(solution)/shard_map/ppermute | solution.py:31
  62.1 9.0 %copy-start.1 = (bf16[1,512,2048]{2,1,0:T(8,128)(2,1)S(1)}, bf16[1,512,2048]{2,1,0:T(8,128)(2,1)}, u32[]{:S(2)}) copy-start(bf16[1,512,2048]{2,1,0:T(8,128)(2,1)} %param.5) | copy-start | bytes 6291460
  65.9 12.1 %collective-permute-start.12 = (bf16[640,128]{1,0:T(8,128)(2,1)S(1)}, bf16[640,128]{1,0:T(8,128)(2,1)S(1)}, u32[]{:S(2)}, u32[]{:S(2)}) collective-permute-start(bf16[640,128]{1,0:T(8,128)(2,1)S(1)} %multiply_convert_fusion.mine_ref), channel_id=1, source_target_pairs={{0,1},{1,0},{2,3},{3,2},{4,5},{5,4},{6,7},{7,6},{8,9},{9,8},{10,11... | collective-permute-start | bytes 491528 | tf_op jit(solution)/shard_map/ppermute | solution.py:41

commit v3 on v2

--- a/solution.py
+++ b/solution.py
@@ -1,3 +1,5 @@
+import functools
+
 import jax
 import jax.numpy as jnp
 from jax import lax
@@ -128,43 +130,75 @@
 
 def first_gamma_kernel(codes, counts, gamma_in, mt_ref, r_ref, gamma_ref):
     own, far = weights(codes, counts, first_round(lax.axis_index("mem")))
-    aux = gamma_ref.shape[1]
-    for p in range(STRIPS):
-        at = pl.ds(p * (aux // STRIPS), aux // STRIPS)
-        gamma_ref[:, at] = gamma_in[:, at] + (own + far) * nn(mt_ref[...], r_ref[:, at])
+    add_gamma(own + far, mt_ref, r_ref, gamma_in, gamma_ref)
+
+
+def strip_loop(count, width, body):
+    def step(p, carry):
+        body(p, pl.ds(pl.multiple_of(p * width, width), width))
+        return carry
+
+    lax.fori_loop(0, count, step, 0)
 
 
 def strips_out(out_ref, held, sems, strips, compute):
-    step = held.shape[1] // strips
-    copies = []
-    for p in range(strips):
-        at = pl.ds(p * step, step)
+    width = held.shape[1] // strips
+
+    def send(p, at):
+        return pltpu.make_async_copy(held.at[:, at], out_ref.at[:, at], sems.at[p])
+
+    def body(p, at):
         held[:, at] = compute(at).astype(held.dtype)
-        copies.append(pltpu.make_async_copy(held.at[:, at], out_ref.at[:, at], sems.at[p]))
-        copies[-1].start()
-    for copy in copies:
-        copy.wait()
-
-
-def second_gamma_kernel(codes, counts, b_ref, over_ref, gamma_in, *refs):
-    parts, (gamma_ref, held) = refs[:-2], refs[-2:]
-    own, far = weights(codes, counts, 3 - first_round(lax.axis_index("mem")))
+        send(p, at).start()
+
+    strip_loop(strips, width, body)
+    strip_loop(strips, width, lambda p, at: send(p, at).wait())
+
+
+def joined(parts, held):
     start = 0
     for part in parts:
         held[start : start + part.shape[0], :] = part[...]
         start += part.shape[0]
-    mt = amp_part(slice(0, start), b_ref, held, over_ref)
+
+
+def add_gamma(weight, mt_ref, r_ref, gamma_in, gamma_ref):
     aux = gamma_ref.shape[1]
-    for p in range(STRIPS):
-        at = pl.ds(p * (aux // STRIPS), aux // STRIPS)
-        gamma_ref[:, at] = gamma_in[:, at] + (own + far) * nn(mt, held[:, at])
-
-
-def last_gamma_kernel(codes, counts, b_ref, over_ref, gamma_in, r_ref, out_ref, held, sems):
+
+    def body(p, at):
+        gamma_ref[:, at] = gamma_in[:, at] + weight * nn(mt_ref[...], r_ref[:, at])
+
+    strip_loop(STRIPS, aux // STRIPS, body)
+
+
+def second_gamma_kernel(codes, counts, b_ref, over_ref, gamma_in, *refs):
+    parts, (gamma_ref, held, mt_ref) = refs[:-3], refs[-3:]
+    own, far = weights(codes, counts, 3 - first_round(lax.axis_index("mem")))
+    joined(parts, held)
+    mt_ref[...] = amp_part(slice(0, held.shape[0]), b_ref, held, over_ref)
+    add_gamma(own + far, mt_ref, held, gamma_in, gamma_ref)
+
+
+def flat_amp(at, b_ref, r_ref, over_ref, m_ref):
+    m_ref[...] = (nt(r_ref[...], b_ref[...]) * over_ref[at, :]).astype(BF16)
+    return m_ref[...].T
+
+
+def third_gamma_kernel(cut, codes, counts, b_ref, over_ref, gamma_in, r_ref, gamma_ref, mt_ref, m_ref):
+    own, far = weights(codes, counts, 3 - first_round(lax.axis_index("mem")))
+    at = slice(cut, cut + r_ref.shape[0])
+    mt_ref[...] = flat_amp(at, b_ref, r_ref, over_ref, m_ref)
+    add_gamma(own + far, mt_ref, r_ref, gamma_in, gamma_ref)
+
+
+def last_gamma_kernel(codes, counts, b_ref, over_ref, gamma_in, r_ref, out_ref, held, sems, mt_ref, m_ref):
     own, far = weights(codes, counts, 3 - first_round(lax.axis_index("mem")))
     vir = b_ref.shape[0]
-    mt = amp_part(slice(vir - r_ref.shape[0], vir), b_ref, r_ref, over_ref)
-    strips_out(out_ref, held, sems, 2, lambda at: gamma_in[:, at] + (own + far) * nn(mt, r_ref[:, at]))
+    at = slice(vir - r_ref.shape[0], vir)
+    mt_ref[...] = flat_amp(at, b_ref, r_ref, over_ref, m_ref)
+    strips_out(
+        out_ref, held, sems, STRIPS, lambda at: gamma_in[:, at] + (own + far) * nn(mt_ref[...], r_ref[:, at])
+    )
 
 
 def apply_kernel(mine_ref, other_ref, b_ref, out_ref, tile, held, sems):
@@ -240,18 +274,26 @@
     other = swap(mine, [(0, 1), (0, 1)])
 
     unit = vir // 32
-    cuts = (0, 7 * unit, 13 * unit, 16 * unit, vir)
+    cuts = (0, 7 * unit, 14 * unit, 16 * unit, 24 * unit, vir)
     parts = [block[a:b] for a, b in zip(cuts, cuts[1:])]
     second = [turn(part, True) for part in parts]
     gamma = call(first_gamma_kernel, wide, (), (0, 1), 5, dot)(
         pair_code, pair_count, gamma, mt, first
     )
     gamma = call(
-        second_gamma_kernel, wide, [pltpu.VMEM((cuts[3], aux), BF16)], (0, 1), 8, dot
+        second_gamma_kernel, wide, [pltpu.VMEM((cuts[3], aux), BF16), pltpu.VMEM((vir, cuts[3]), BF16)],
+        (0, 1), 8, dot,
     )(pair_code, pair_count, block, over_second, gamma, *second[:3])
+    third, last = cuts[4] - cuts[3], vir - cuts[4]
+    gamma = call(
+        functools.partial(third_gamma_kernel, cuts[3]), wide,
+        [pltpu.VMEM((vir, third), BF16), pltpu.VMEM((third, vir), BF16)], (0, 1), 6, dot // 2,
+    )(pair_code, pair_count, block, over_second, gamma, second[3])
     result = call(
-        last_gamma_kernel, shape((vir, aux), BF16), out_scratch, (0, 1), 6, dot, any_space
-    )(pair_code, pair_count, block, over_second, gamma, second[3])
+        last_gamma_kernel, shape((vir, aux), BF16),
+        [*out_scratch, pltpu.VMEM((vir, last), BF16), pltpu.VMEM((last, vir), BF16)],
+        (0, 1), 6, dot // 2, any_space,
+    )(pair_code, pair_count, block, over_second, gamma, second[4])
     lagrangian = call(
         apply_kernel, shape((vir, aux), BF16), [pltpu.VMEM((vir, vir), BF16), *out_scratch], (), 3, dot,
         any_space,

time: 80.4 us -> 87.7 us (1.091)
  starting transfers between devices: 11 us -> 14.2 us
  Pallas kernels: 16.9 us -> 19.8 us
  waiting for transfers between devices: 45.4 us -> 46.5 us
    ppermute x7 -> x8, waiting for transfers between devices: 27.1 us -> 33.8 us  [turn(): return lax.ppermute(value, 'mem', pairs)]
    ppermute x6, waiting for transfers between devices: 18.3 us -> 12.7 us  [swap(): return lax.ppermute(value, ('grp', 'mem'), pairs)]
    pallas_call x6 -> x7, Pallas kernels: 16.9 us -> 19.8 us  [call(): kernel_call(kernel, outs, scratch, smem, count, flops, out_spec)(*args)]
    ppermute x6, starting transfers between devices: 6.04 us -> 7.99 us  [swap(): return lax.ppermute(value, ('grp', 'mem'), pairs)]
    ppermute x7 -> x8, starting transfers between devices: 4.92 us -> 6.24 us  [turn(): return lax.ppermute(value, 'mem', pairs)]
    unnamed x7 -> x9, local copies, waits for them, and re-layouts: 3 us -> 3.01 us
  transfers between devices with their start and end apart: 13 -> 14, of which waited for: 7 -> 7; matrix products, arithmetic and copies ran while one was open for 2% -> 2% of each run, Pallas kernels for 15% -> 17%
where the time goes in v3:
time: 87.7 us; the launch traced here: 87.4 us
  waiting for transfers between devices  46.5 us (53%)
  Pallas kernels  19.8 us (23%)
  starting transfers between devices  14.2 us (16%)
  local copies, waits for them, and re-layouts  3.15 us (4%)
  between operations  2.77 us (3%)
  other arithmetic  0.97 us (1%)
    ppermute x8, waiting for transfers between devices, turn(): return lax.ppermute(value, 'mem', pairs)  33.8 us
    pallas_call x7, Pallas kernels, call(): kernel_call(kernel, outs, scratch, smem, count, flops, out_spec)(*args)  19.8 us
    ppermute x6, waiting for transfers between devices, swap(): return lax.ppermute(value, ('grp', 'mem'), pairs)  12.7 us
    ppermute x6, starting transfers between devices, swap(): return lax.ppermute(value, ('grp', 'mem'), pairs)  7.99 us
    ppermute x8, starting transfers between devices, turn(): return lax.ppermute(value, 'mem', pairs)  6.24 us
    unnamed x9, local copies, waits for them, and re-layouts  3.01 us
  transfers between devices with their start and end apart: 14, of which 7 were waited for; matrix products, arithmetic and copies ran while one was open for 2% of the time, Pallas kernels for 17%

profile of v3, /device:TPU:0, one launch (start us, length us, event | category | flops | bytes accessed | tf_op | source)
XLA Modules:
  0.0 87.4 jit_solution(17558810389523429723)
XLA Ops:
  0.6 0.6 collective-permute-start.2
  1.2 2.1 %collective-permute-start = (bf16[1]{0:T(256)(128)(2,1)}, bf16[1]{0:T(256)(128)(2,1)}, u32[]{:S(2)}, u32[]{:S(2)}) collective-permute-start(bf16[1]{0:T(256)(128)(2,1)} %param.6), channel_id=1, source_target_pairs={{0,1},{1,3},{2,0},{3,2},{4,5},{5,7},{6,4},{7,6},{8,9},{9,11},{10,8... | collective-permute-start | bytes 14 | tf_op jit(solution)/shard_map/ppermute | solution.py:33
  3.3 0.6 collective-permute-start.1
  4.6 0.8 copy.12.codes
  5.3 0.7 reshape.16
  6.0 22.0 %collective-permute-done = bf16[1]{0:T(256)(128)(2,1)} collective-permute-done((bf16[1]{0:T(256)(128)(2,1)}, bf16[1]{0:T(256)(128)(2,1)}, u32[]{:S(2)}, u32[]{:S(2)}) %collective-permute-start) | collective-permute-done | bytes 34 | tf_op jit(solution)/shard_map/ppermute | solution.py:33
  28.7 0.0 collective-permute-done.1
  29.3 0.0 copy-start
  29.3 1.6 %copy-done = bf16[1,512,2048]{2,1,0:T(8,128)(2,1)S(1)} copy-done((bf16[1,512,2048]{2,1,0:T(8,128)(2,1)S(1)}, bf16[1,512,2048]{2,1,0:T(8,128)(2,1)}, u32[]{:S(2)}) %copy-start) | copy-done | bytes 2097176
  30.9 0.7 copy-done.2
  31.5 3.5 %shard_map.68 = (f32[512,512]{1,0:T(8,128)S(1)}, f32[512,512]{1,0:T(8,128)S(1)}, f32[512,512]{1,0:T(8,128)S(1)}, f32[512,2048]{1,0:T(8,128)S(1)}) custom-call(bf16[512,2048]{1,0:T(8,128)(2,1)S(1)} %bitcast.15, f32[1,512]{1,0:T(1,128)S(1)} %bitcast.21, f32[1]{0:T(128)S(6)} %convert_element_type.40.e_ref, f32[1]{0:T(128)S(6)} %convert_element_type.41.first_ref, ...), custom_call_target="tpu_custom_call" | custom-call | flops 2147483648 | bytes 1048576 | tf_op jit(solution)/shard_map/pallas_call | solution.py:219
  35.0 0.0 collective-permute-done.2.r_ref
  35.0 2.5 %shard_map.69 = (bf16[512,512]{1,0:T(8,128)(2,1)S(1)}, f32[640,128]{1,0:T(8,128)S(1)}, bf16[640,128]{1,0:T(8,128)(2,1)S(1)}) custom-call(bf16[512,2048]{1,0:T(8,128)(2,1)S(1)} %bitcast.16, bf16[512,2048]{1,0:T(8,128)(2,1)S(1)} %collective-permute-done.2.r_ref, f32[512,512]{1,0:T(8,128)S(1)} %get-tuple-element.11.over_ref, s32[1,8,3]{2,1,0:T(8,128)S(1)} %copy.12.codes, ...), custom_call_target="tpu_custom_call" | custom-call | flops 1073741824 | bytes 1048576 | tf_op jit(solution)/shard_map/pallas_call | solution.py:219
  37.5 0.1 collective-permute-start.8
  37.6 1.4 %collective-permute-done.8 = bf16[640,128]{1,0:T(8,128)(2,1)S(1)} collective-permute-done((bf16[640,128]{1,0:T(8,128)(2,1)S(1)}, bf16[640,128]{1,0:T(8,128)(2,1)S(1)}, u32[]{:S(2)}, u32[]{:S(2)}) %collective-permute-start.8) | collective-permute-done | bytes 163872 | tf_op jit(solution)/shard_map/ppermute | solution.py:43
  39.0 0.4 collective-permute-start.9
  39.5 5.8 %collective-permute-done.9 = bf16[640,128]{1,0:T(8,128)(2,1)S(1)} collective-permute-done((bf16[640,128]{1,0:T(8,128)(2,1)S(1)}, bf16[640,128]{1,0:T(8,128)(2,1)S(1)}, u32[]{:S(2)}, u32[]{:S(2)}) %collective-permute-start.9) | collective-permute-done | bytes 163872 | tf_op jit(solution)/shard_map/ppermute | solution.py:43
  45.3 0.1 fusion.3
  45.4 2.3 %collective-permute-start.10 = (bf16[640,128]{1,0:T(8,128)(2,1)S(1)}, bf16[640,128]{1,0:T(8,128)(2,1)S(1)}, u32[]{:S(2)}, u32[]{:S(2)}) collective-permute-start(bf16[640,128]{1,0:T(8,128)(2,1)S(1)} %get-tuple-element.16), channel_id=1, source_target_pairs={{0,7},{1,17},{2,18},{3,4},{4,3},{5,21},{6,22},{7,0},{8,15},{9,25},... | collective-permute-start | bytes 491528 | tf_op jit(solution)/shard_map/ppermute | solution.py:43
  47.7 0.1 slice_bitcast_fusion.2
  47.7 0.0 copy-start.3
  47.7 0.1 collective-permute-start.3
  47.8 1.4 %collective-permute-start.4 = (bf16[112,2048]{1,0:T(8,128)(2,1)S(1)}, bf16[112,2048]{1,0:T(8,128)(2,1)S(1)}, u32[]{:S(2)}, u32[]{:S(2)}) collective-permute-start(bf16[112,2048]{1,0:T(8,128)(2,1)S(1)} %get-tuple-element.20), channel_id=1, source_target_pairs={{1,0},{3,1},{0,2},{2,3},{5,4},{7,5},{4,6},{6,7},{9,8},{11,9},{8,10... | collective-permute-start | bytes 1376264 | tf_op jit(solution)/shard_map/ppermute | solution.py:33
  49.3 2.8 %collective-permute-done.10 = bf16[640,128]{1,0:T(8,128)(2,1)S(1)} collective-permute-done((bf16[640,128]{1,0:T(8,128)(2,1)S(1)}, bf16[640,128]{1,0:T(8,128)(2,1)S(1)}, u32[]{:S(2)}, u32[]{:S(2)}) %collective-permute-start.10) | collective-permute-done | bytes 163872 | tf_op jit(solution)/shard_map/ppermute | solution.py:43
  52.1 2.0 %collective-permute-start.11 = (bf16[640,128]{1,0:T(8,128)(2,1)S(1)}, bf16[640,128]{1,0:T(8,128)(2,1)S(1)}, u32[]{:S(2)}, u32[]{:S(2)}) collective-permute-start(bf16[640,128]{1,0:T(8,128)(2,1)S(1)} %fusion.1), channel_id=1, source_target_pairs={{0,8},{1,6},{2,5},{3,11},{4,12},{5,2},{6,1},{7,15},{8,0},{9,14},{1... | collective-permute-start | bytes 491528 | tf_op jit(solution)/shard_map/ppermute | solution.py:43
  54.1 0.1 slice_bitcast_fusion
  54.2 0.1 collective-permute-start.6
  54.2 1.4 %collective-permute-start.7 = (bf16[128,2048]{1,0:T(8,128)(2,1)S(1)}, bf16[128,2048]{1,0:T(8,128)(2,1)S(1)}, u32[]{:S(2)}, u32[]{:S(2)}) collective-permute-start(bf16[128,2048]{1,0:T(8,128)(2,1)S(1)} %get-tuple-element.18), channel_id=1, source_target_pairs={{1,0},{3,1},{0,2},{2,3},{5,4},{7,5},{4,6},{6,7},{9,8},{11,9},{8,10... | collective-permute-start | bytes 1572872 | tf_op jit(solution)/shard_map/ppermute | solution.py:33
  55.6 1.9 %collective-permute-done.11 = bf16[640,128]{1,0:T(8,128)(2,1)S(1)} collective-permute-done((bf16[640,128]{1,0:T(8,128)(2,1)S(1)}, bf16[640,128]{1,0:T(8,128)(2,1)S(1)}, u32[]{:S(2)}, u32[]{:S(2)}) %collective-permute-start.11) | collective-permute-done | bytes 163872 | tf_op jit(solution)/shard_map/ppermute | solution.py:43
  57.5 0.1 fusion.2
  57.5 2.0 %collective-permute-start.12 = (bf16[640,128]{1,0:T(8,128)(2,1)S(1)}, bf16[640,128]{1,0:T(8,128)(2,1)S(1)}, u32[]{:S(2)}, u32[]{:S(2)}) collective-permute-start(bf16[640,128]{1,0:T(8,128)(2,1)S(1)} %fusion.2), channel_id=1, source_target_pairs={{0,16},{1,9},{2,10},{3,19},{4,20},{5,13},{6,14},{7,23},{8,24},{9,1... | collective-permute-start | bytes 491528 | tf_op jit(solution)/shard_map/ppermute | solution.py:43
  59.6 0.0 copy-done.3
  59.6 0.0 copy-start.1
  59.6 2.4 %shard_map.70.gamma_in = f32[512,2048]{1,0:T(8,128)S(1)} custom-call(s32[1,8,3]{2,1,0:T(8,128)S(1)} %copy.12.codes, s32[1,8]{1,0:T(1,128)S(1)} %copy-done.3, f32[512,2048]{1,0:T(8,128)S(1)} %get-tuple-element.10.gamma_in, bf16[512,512]{1,0:T(8,128)(2,1)S(1)} %get-tuple-element.13.mt_ref, bf16[512,2048]{1,0:T(8,128)(2,1)S(1)} %collective-permute-done.2.r_ref), custom_call_target="tpu_custom_call" | custom-call | flops 1073741824 | bytes 1048576 | tf_op jit(solution)/shard_map/pallas_call | solution.py:219
  62.0 0.9 %collective-permute-done.12 = bf16[640,128]{1,0:T(8,128)(2,1)S(1)} collective-permute-done((bf16[640,128]{1,0:T(8,128)(2,1)S(1)}, bf16[640,128]{1,0:T(8,128)(2,1)S(1)}, u32[]{:S(2)}, u32[]{:S(2)}) %collective-permute-start.12) | collective-permute-done | bytes 163872 | tf_op jit(solution)/shard_map/ppermute | solution.py:43
  62.9 0.0 collective-permute-start.5
  62.9 0.1 multiply_convert_fusion.mine_ref
  63.0 11.8 %collective-permute-done.5.refs_2_ = bf16[32,2048]{1,0:T(8,128)(2,1)S(1)} collective-permute-done((bf16[32,2048]{1,0:T(8,128)(2,1)S(1)}, bf16[32,2048]{1,0:T(8,128)(2,1)S(1)}, u32[]{:S(2)}, u32[]{:S(2)}) %collective-permute-start.5) | collective-permute-done | bytes 131104 | tf_op jit(solution)/shard_map/ppermute | solution.py:33
  74.8 1.1 %collective-permute-start.13 = (bf16[640,128]{1,0:T(8,128)(2,1)S(1)}, bf16[640,128]{1,0:T(8,128)(2,1)S(1)}, u32[]{:S(2)}, u32[]{:S(2)}) collective-permute-start(bf16[640,128]{1,0:T(8,128)(2,1)S(1)} %multiply_convert_fusion.mine_ref), channel_id=1, source_target_pairs={{0,1},{1,0},{2,3},{3,2},{4,5},{5,4},{6,7},{7,6},{8,9},{9,8},{10,11... | collective-permute-start | bytes 491528 | tf_op jit(solution)/shard_map/ppermute | solution.py:43
  75.9 0.0 collective-permute-done.3.refs_0_
  75.9 0.0 collective-permute-done.4.refs_1_
  75.9 2.6 %shard_map.71.gamma_in = f32[512,2048]{1,0:T(8,128)S(1)} custom-call(s32[1,8,3]{2,1,0:T(8,128)S(1)} %copy.12.codes, s32[1,8]{1,0:T(1,128)S(1)} %copy-done.3, bf16[512,2048]{1,0:T(8,128)(2,1)S(1)} %bitcast.17, f32[512,512]{1,0:T(8,128)S(1)} %get-tuple-element.9.over_ref, f32[512,2048]{1,0:T(8,128)S(1)} %shard_map.70.gamma_in, ...), custom_call_target="tpu_custom_call" | custom-call | flops 1073741824 | bytes 1048576 | tf_op jit(solution)/shard_map/pallas_call | solution.py:219
  78.5 0.0 collective-permute-done.6.r_ref
  78.5 2.6 %shard_map.72.gamma_in = f32[512,2048]{1,0:T(8,128)S(1)} custom-call(s32[1,8,3]{2,1,0:T(8,128)S(1)} %copy.12.codes, s32[1,8]{1,0:T(1,128)S(1)} %copy-done.3, bf16[512,2048]{1,0:T(8,128)(2,1)S(1)} %bitcast.18, f32[512,512]{1,0:T(8,128)S(1)} %get-tuple-element.9.over_ref, f32[512,2048]{1,0:T(8,128)S(1)} %shard_map.71.gamma_in, ...), custom_call_target="tpu_custom_call" | custom-call | flops 536870912 | bytes 1048576 | tf_op jit(solution)/shard_map/pallas_call | solution.py:219
  81.2 0.0 collective-permute-done.7.r_ref
  81.2 3.5 %shard_map.73 = bf16[512,2048]{1,0:T(8,128)(2,1)} custom-call(s32[1,8,3]{2,1,0:T(8,128)S(1)} %copy.12.codes, s32[1,8]{1,0:T(1,128)S(1)} %copy-done.3, bf16[512,2048]{1,0:T(8,128)(2,1)S(1)} %bitcast.19, f32[512,512]{1,0:T(8,128)S(1)} %get-tuple-element.9.over_ref, f32[512,2048]{1,0:T(8,128)S(1)} %shard_map.72.gamma_in, ...), custom_call_target="tpu_custom_call" | custom-call | flops 536870912 | bytes 1048576 | tf_op jit(solution)/shard_map/pallas_call | solution.py:219
  84.7 0.0 collective-permute-done.13.other_ref
  84.7 2.7 %shard_map.74 = bf16[512,2048]{1,0:T(8,128)(2,1)} custom-call(bf16[640,128]{1,0:T(8,128)(2,1)S(1)} %multiply_convert_fusion.mine_ref, bf16[640,128]{1,0:T(8,128)(2,1)S(1)} %collective-permute-done.13.other_ref, bf16[512,2048]{1,0:T(8,128)(2,1)S(1)} %bitcast.20), custom_call_target="tpu_custom_call" | custom-call | flops 1073741824 | bytes 1048576 | tf_op jit(solution)/shard_map/pallas_call | solution.py:219
  (5 shorter events, 0.1 us)
Async XLA Ops:
  0.6 34.4 %collective-permute-start.2 = (bf16[512,2048]{1,0:T(8,128)(2,1)}, bf16[512,2048]{1,0:T(8,128)(2,1)S(1)}, u32[]{:S(2)}, u32[]{:S(2)}) collective-permute-start(bf16[512,2048]{1,0:T(8,128)(2,1)} %bitcast.14), channel_id=1, source_target_pairs={{0,1},{1,3},{2,0},{3,2},{4,5},{5,7},{6,4},{7,6},{8,9},{9,11},{10,8... | collective-permute-start | bytes 6291464 | tf_op jit(solution)/shard_map/ppermute | solution.py:33
  1.2 26.8 %collective-permute-start = (bf16[1]{0:T(256)(128)(2,1)}, bf16[1]{0:T(256)(128)(2,1)}, u32[]{:S(2)}, u32[]{:S(2)}) collective-permute-start(bf16[1]{0:T(256)(128)(2,1)} %param.6), channel_id=1, source_target_pairs={{0,1},{1,3},{2,0},{3,2},{4,5},{5,7},{6,4},{7,6},{8,9},{9,11},{10,8... | collective-permute-start | bytes 14 | tf_op jit(solution)/shard_map/ppermute | solution.py:33
  3.3 25.4 %collective-permute-start.1 = (bf16[1]{0:T(256)(128)(2,1)}, bf16[1]{0:T(256)(128)(2,1)}, u32[]{:S(2)}, u32[]{:S(2)}) collective-permute-start(bf16[1]{0:T(256)(128)(2,1)} %param.6), channel_id=1, source_target_pairs={{1,0},{3,1},{0,2},{2,3},{5,4},{7,5},{4,6},{6,7},{9,8},{11,9},{8,10... | collective-permute-start | bytes 14 | tf_op jit(solution)/shard_map/ppermute | solution.py:33
  29.3 1.6 %copy-start = (bf16[1,512,2048]{2,1,0:T(8,128)(2,1)S(1)}, bf16[1,512,2048]{2,1,0:T(8,128)(2,1)}, u32[]{:S(2)}) copy-start(bf16[1,512,2048]{2,1,0:T(8,128)(2,1)} %param.5) | copy-start | bytes 6291460
  30.9 0.7 copy-start.2
  37.5 1.5 %collective-permute-start.8 = (bf16[640,128]{1,0:T(8,128)(2,1)S(1)}, bf16[640,128]{1,0:T(8,128)(2,1)S(1)}, u32[]{:S(2)}, u32[]{:S(2)}) collective-permute-start(bf16[640,128]{1,0:T(8,128)(2,1)S(1)} %get-tuple-element.15), channel_id=1, source_target_pairs={{0,1},{1,0},{2,3},{3,2},{4,5},{5,4},{6,7},{7,6},{8,9},{9,8},{10,11... | collective-permute-start | bytes 491528 | tf_op jit(solution)/shard_map/ppermute | solution.py:43
  39.0 6.2 %collective-permute-start.9 = (bf16[640,128]{1,0:T(8,128)(2,1)S(1)}, bf16[640,128]{1,0:T(8,128)(2,1)S(1)}, u32[]{:S(2)}, u32[]{:S(2)}) collective-permute-start(bf16[640,128]{1,0:T(8,128)(2,1)S(1)} %fusion), channel_id=1, source_target_pairs={{0,3},{1,2},{2,1},{3,0},{4,7},{5,6},{6,5},{7,4},{8,11},{9,10},{10,... | collective-permute-start | bytes 491528 | tf_op jit(solution)/shard_map/ppermute | solution.py:43
  45.4 6.7 %collective-permute-start.10 = (bf16[640,128]{1,0:T(8,128)(2,1)S(1)}, bf16[640,128]{1,0:T(8,128)(2,1)S(1)}, u32[]{:S(2)}, u32[]{:S(2)}) collective-permute-start(bf16[640,128]{1,0:T(8,128)(2,1)S(1)} %get-tuple-element.16), channel_id=1, source_target_pairs={{0,7},{1,17},{2,18},{3,4},{4,3},{5,21},{6,22},{7,0},{8,15},{9,25},... | collective-permute-start | bytes 491528 | tf_op jit(solution)/shard_map/ppermute | solution.py:43
  47.7 11.9 %copy-start.3 = (s32[1,8]{1,0:T(1,128)S(1)}, s32[1,8]{1,0:T(1,128)}, u32[]{:S(2)}) copy-start(s32[1,8]{1,0:T(1,128)} %counts.11) | copy-start | bytes 100
  47.7 28.2 %collective-permute-start.3 = (bf16[112,2048]{1,0:T(8,128)(2,1)S(1)}, bf16[112,2048]{1,0:T(8,128)(2,1)S(1)}, u32[]{:S(2)}, u32[]{:S(2)}) collective-permute-start(bf16[112,2048]{1,0:T(8,128)(2,1)S(1)} %get-tuple-element.21), channel_id=1, source_target_pairs={{1,0},{3,1},{0,2},{2,3},{5,4},{7,5},{4,6},{6,7},{9,8},{11,9},{8,10... | collective-permute-start | bytes 1376264 | tf_op jit(solution)/shard_map/ppermute | solution.py:33
  47.8 28.1 %collective-permute-start.4 = (bf16[112,2048]{1,0:T(8,128)(2,1)S(1)}, bf16[112,2048]{1,0:T(8,128)(2,1)S(1)}, u32[]{:S(2)}, u32[]{:S(2)}) collective-permute-start(bf16[112,2048]{1,0:T(8,128)(2,1)S(1)} %get-tuple-element.20), channel_id=1, source_target_pairs={{1,0},{3,1},{0,2},{2,3},{5,4},{7,5},{4,6},{6,7},{9,8},{11,9},{8,10... | collective-permute-start | bytes 1376264 | tf_op jit(solution)/shard_map/ppermute | solution.py:33
  52.1 5.4 %collective-permute-start.11 = (bf16[640,128]{1,0:T(8,128)(2,1)S(1)}, bf16[640,128]{1,0:T(8,128)(2,1)S(1)}, u32[]{:S(2)}, u32[]{:S(2)}) collective-permute-start(bf16[640,128]{1,0:T(8,128)(2,1)S(1)} %fusion.1), channel_id=1, source_target_pairs={{0,8},{1,6},{2,5},{3,11},{4,12},{5,2},{6,1},{7,15},{8,0},{9,14},{1... | collective-permute-start | bytes 491528 | tf_op jit(solution)/shard_map/ppermute | solution.py:43
  54.2 24.3 %collective-permute-start.6 = (bf16[128,2048]{1,0:T(8,128)(2,1)S(1)}, bf16[128,2048]{1,0:T(8,128)(2,1)S(1)}, u32[]{:S(2)}, u32[]{:S(2)}) collective-permute-start(bf16[128,2048]{1,0:T(8,128)(2,1)S(1)} %get-tuple-element.19), channel_id=1, source_target_pairs={{1,0},{3,1},{0,2},{2,3},{5,4},{7,5},{4,6},{6,7},{9,8},{11,9},{8,10... | collective-permute-start | bytes 1572872 | tf_op jit(solution)/shard_map/ppermute | solution.py:33
  54.2 26.9 %collective-permute-start.7 = (bf16[128,2048]{1,0:T(8,128)(2,1)S(1)}, bf16[128,2048]{1,0:T(8,128)(2,1)S(1)}, u32[]{:S(2)}, u32[]{:S(2)}) collective-permute-start(bf16[128,2048]{1,0:T(8,128)(2,1)S(1)} %get-tuple-element.18), channel_id=1, source_target_pairs={{1,0},{3,1},{0,2},{2,3},{5,4},{7,5},{4,6},{6,7},{9,8},{11,9},{8,10... | collective-permute-start | bytes 1572872 | tf_op jit(solution)/shard_map/ppermute | solution.py:33
  57.5 5.4 %collective-permute-start.12 = (bf16[640,128]{1,0:T(8,128)(2,1)S(1)}, bf16[640,128]{1,0:T(8,128)(2,1)S(1)}, u32[]{:S(2)}, u32[]{:S(2)}) collective-permute-start(bf16[640,128]{1,0:T(8,128)(2,1)S(1)} %fusion.2), channel_id=1, source_target_pairs={{0,16},{1,9},{2,10},{3,19},{4,20},{5,13},{6,14},{7,23},{8,24},{9,1... | collective-permute-start | bytes 491528 | tf_op jit(solution)/shard_map/ppermute | solution.py:43
  59.6 16.3 %copy-start.1 = (bf16[1,512,2048]{2,1,0:T(8,128)(2,1)S(1)}, bf16[1,512,2048]{2,1,0:T(8,128)(2,1)}, u32[]{:S(2)}) copy-start(bf16[1,512,2048]{2,1,0:T(8,128)(2,1)} %param.5) | copy-start | bytes 6291460
  62.9 11.8 %collective-permute-start.5 = (bf16[32,2048]{1,0:T(8,128)(2,1)S(1)}, bf16[32,2048]{1,0:T(8,128)(2,1)S(1)}, u32[]{:S(2)}, u32[]{:S(2)}) collective-permute-start(bf16[32,2048]{1,0:T(8,128)(2,1)S(1)} %slice_bitcast_fusion.4), channel_id=1, source_target_pairs={{1,0},{3,1},{0,2},{2,3},{5,4},{7,5},{4,6},{6,7},{9,8},{11,9},{8,10... | collective-permute-start | bytes 393224 | tf_op jit(solution)/shard_map/ppermute | solution.py:33
  74.8 9.9 %collective-permute-start.13 = (bf16[640,128]{1,0:T(8,128)(2,1)S(1)}, bf16[640,128]{1,0:T(8,128)(2,1)S(1)}, u32[]{:S(2)}, u32[]{:S(2)}) collective-permute-start(bf16[640,128]{1,0:T(8,128)(2,1)S(1)} %multiply_convert_fusion.mine_ref), channel_id=1, source_target_pairs={{0,1},{1,0},{2,3},{3,2},{4,5},{5,4},{6,7},{7,6},{8,9},{9,8},{10,11... | collective-permute-start | bytes 491528 | tf_op jit(solution)/shard_map/ppermute | solution.py:43
